TPU v7x, 32 devices: a whole 2x2x4 slice. The times are simulated.
32 devices in a mesh: dp: 16 (over z, y, x), mp: 2 (over core).
Axes of the slice: x: 2, y: 2, z: 4, core: 2. Of those that a mesh axis runs over, the one named last changes fastest.
Arguments:
- log_rows: bfloat16 [98304, 256], P('dp'), may hold values from -6 to 6
- query_ids: int32 [98304], P('dp'), may hold values from 0 to 191, as said below
- doc_ranks: int32 [98304], P('dp'), may hold values from 0 to 511, as said below
- row_counts: int32 [16, 16], P('dp'), may hold values from 0 to 384, as said below
- list_lengths: int32 [192], P('dp'), may hold values from 64 to 512, as said below
- gains: float32 [192, 512], P('dp'), may hold values from 0.01 to 1
- weight_in: float32 [256, 4096], P(None, 'mp'), may hold values from -0.375 to 0.375
- bias_in: float32 [4096], P('mp'), may hold values from -3 to 3
- weight_out: float32 [4096], P('mp'), may hold values from -0.3 to 0.3
- moment_w: float32 [256, 4096], P(None, 'mp'), may hold values from -0.6 to 0.6
- second_w: float32 [256, 4096], P(None, 'mp'), may hold values from 0.05 to 2
- moment_b: float32 [4096], P('mp'), may hold values from -0.6 to 0.6
- second_b: float32 [4096], P('mp'), may hold values from 0.05 to 2
- moment_o: float32 [4096], P('mp'), may hold values from -0.6 to 0.6
- second_o: float32 [4096], P('mp'), may hold values from 0.05 to 2
Outputs:
- doc_lambdas: float32 [192, 512], P('dp')
- weight_in_next: float32 [256, 4096], P(None, 'mp')
- moment_w_next: float32 [256, 4096], P(None, 'mp')
- second_w_next: float32 [256, 4096], P(None, 'mp')
- bias_in_next: float32 [4096], P('mp')
- moment_b_next: float32 [4096], P('mp')
- second_b_next: float32 [4096], P('mp')
- weight_out_next: float32 [4096], P('mp')
- moment_o_next: float32 [4096], P('mp')
- second_o_next: float32 [4096], P('mp')
Inputs may be any that keep to these rules, and one draw needn't show every extreme that they name: row_counts[s, j] is at most 384; the live rows that all shards hold for owner j number list_lengths summed over owner j's queries j * 12 to j * 12 + 11; some owner receives 384 live rows from every shard. `query_ids`: A live row of the block for owner j belongs to one of owner j's queries; rows that are not live carry arbitrary ids. `doc_ranks`: the live rows of query q carry the ranks 0 to list_lengths[q] - 1, each once; rows that are not live carry arbitrary ranks. `list_lengths`: every owner has a list of 512 documents.
All inputs are finite; a program needn't handle non-finite values.
Results may differ from a plain program's by a relative error of at most 0.0049.
Values may be sent and summed in bfloat16 or wider, within the bound.
A program may use at most 192 MiB of HBM per device.

v0:
```python
import jax
import jax.numpy as jnp
from jax import lax
from jax.sharding import PartitionSpec as P

beta_one = 0.9
beta_two = 0.95
learn_rate = 0.001
adam_eps = 1e-08


def gelu_tanh(values):
    return jax.nn.gelu(values, approximate=True)


def owner_lambdas(score_rows, gain_rows, lengths):
    list_width = gain_rows.shape[1]
    positions = jnp.arange(list_width)
    discount = 1.0 / jnp.log2(2.0 + positions.astype(jnp.float32))
    keep_mask = (positions[None, :] < lengths[:, None]).astype(jnp.float32)

    def per_list(triple):
        row_score, row_gain, row_keep = triple
        delta_s = row_score[:, None] - row_score[None, :]
        delta_g = row_gain[:, None] - row_gain[None, :]
        weight = (
            jnp.abs(discount[:, None] - discount[None, :]) * row_keep[:, None] * row_keep[None, :]
        )
        pair_term = jnp.maximum(delta_g, 0.0) * jax.nn.sigmoid(-delta_s) - jnp.maximum(
            -delta_g, 0.0
        ) * jax.nn.sigmoid(delta_s)
        return -jnp.sum(weight * pair_term, axis=1)

    return lax.map(per_list, (score_rows, gain_rows, keep_mask))


def adam_step(weights, moment, second, gradient):
    moment_next = beta_one * moment + (1.0 - beta_one) * gradient
    second_next = beta_two * second + (1.0 - beta_two) * gradient * gradient
    weights_next = weights - learn_rate * moment_next / (jnp.sqrt(second_next) + adam_eps)
    return (weights_next, moment_next, second_next)


def per_device(
    log_rows,
    query_ids,
    doc_ranks,
    row_counts,
    list_lengths,
    gains,
    weight_in,
    bias_in,
    weight_out,
    moment_w,
    second_w,
    moment_b,
    second_b,
    moment_o,
    second_o,
):
    shard_count = lax.axis_size("dp")
    features = log_rows.shape[1]
    slot_count = log_rows.shape[0] // shard_count
    list_count, list_width = gains.shape
    owner_rows = list_count * list_width
    query_total = list_count * shard_count
    blocks = log_rows.reshape(shard_count, slot_count, features)
    is_live = jnp.arange(slot_count)[None, :] < row_counts.reshape(shard_count, 1)
    targets = jnp.where(
        is_live,
        query_ids.reshape(shard_count, slot_count) % list_count * list_width
        + doc_ranks.reshape(shard_count, slot_count),
        owner_rows,
    )
    w_low = weight_in.astype(jnp.bfloat16)
    arrived = lax.all_to_all(blocks, "dp", split_axis=0, concat_axis=0, tiled=True)
    arrived_slots = lax.all_to_all(targets, "dp", split_axis=0, concat_axis=0, tiled=True)
    used_rows = (
        jnp.zeros((owner_rows, features), jnp.bfloat16)
        .at[arrived_slots.reshape(-1)]
        .set(arrived.reshape(-1, features), mode="drop")
    )
    pre_act = jnp.dot(used_rows, w_low, preferred_element_type=jnp.float32) + bias_in
    hidden, gelu_back = jax.vjp(gelu_tanh, pre_act)
    scores = lax.psum(jnp.sum(hidden * weight_out, axis=1), "mp")
    lambdas = owner_lambdas(scores.reshape(list_count, list_width), gains, list_lengths)
    row_lambdas = lambdas.reshape(-1) / query_total
    grad_pre = gelu_back(row_lambdas[:, None] * weight_out)[0]
    grad_w = lax.dot_general(
        used_rows,
        grad_pre.astype(jnp.bfloat16),
        (((0,), (0,)), ((), ())),
        preferred_element_type=jnp.float32,
    )
    grad_b = jnp.sum(grad_pre, axis=0)
    grad_o = jnp.sum(row_lambdas[:, None] * hidden, axis=0)
    grad_w, grad_b, grad_o = lax.psum((grad_w, grad_b, grad_o), "dp")
    weight_next, moment_w_next, second_w_next = adam_step(weight_in, moment_w, second_w, grad_w)
    bias_next, moment_b_next, second_b_next = adam_step(bias_in, moment_b, second_b, grad_b)
    out_next, moment_o_next, second_o_next = adam_step(weight_out, moment_o, second_o, grad_o)
    return (
        lambdas,
        weight_next,
        moment_w_next,
        second_w_next,
        bias_next,
        moment_b_next,
        second_b_next,
        out_next,
        moment_o_next,
        second_o_next,
    )


def solution(mesh):
    placed = (
        P("dp", None),
        P("dp"),
        P("dp"),
        P("dp", None),
        P("dp"),
        P("dp", None),
        P(None, "mp"),
        P("mp"),
        P("mp"),
        P(None, "mp"),
        P(None, "mp"),
        P("mp"),
        P("mp"),
        P("mp"),
        P("mp"),
    )
    return jax.shard_map(
        per_device,
        mesh=mesh,
        in_specs=placed,
        out_specs=(
            P("dp", None),
            P(None, "mp"),
            P(None, "mp"),
            P(None, "mp"),
            P("mp"),
            P("mp"),
            P("mp"),
            P("mp"),
            P("mp"),
            P("mp"),
        ),
        check_vma=False,
    )
```

profile of v0, /device:TPU:0, one launch (start us, length us, event | category | flops | bytes accessed | tf_op | source)
XLA Modules:
  0.0 381.7 jit_solution(12026352199556250524)
XLA Ops:
  8.8 15.5 %all_to_all.11 = s32[16,1,384]{2,1,0:T(1,128)S(1)} all-to-all(s32[16,1,384]{2,1,0:T(1,128)S(1)} %compare_select_fusion.1), channel_id=1, replica_groups=mesh['dp'=16,'mp'=2] {'dp'}, dimensions={0} | all-to-all | bytes 49152 | tf_op jit(solution)/shard_map/all_to_all | solution.py:77
  24.2 3.7 all-to-all-start.1
  28.8 59.5 %all-to-all-done.1 = bf16[16,384,256]{2,1,0:T(8,128)(2,1)S(1)} async-done(((bf16[16,384,256]{2,1,0:T(8,128)(2,1)}), bf16[16,384,256]{2,1,0:T(8,128)(2,1)S(1)}, u32[]{:S(2)}, u32[]{:S(2)}) %all-to-all-start.1) | async-done | bytes 3145760 | tf_op jit(solution)/shard_map/all_to_all | solution.py:76
  88.3 1.7 copy-done
  89.9 27.8 %scatter_custom_fusion = bf16[6144,256]{1,0:T(8,128)(2,1)S(1)} fusion(s32[6144]{0:T(1024)S(1)} %bitcast.31, bf16[6144,256]{1,0:T(8,128)(2,1)} %bitcast.24, bf16[]{:T(256)} %constant.12.clone.1), kind=kCustom, calls=%fused_computation.43 | custom fusion | bytes 3146240 | tf_op jit(solution)/shard_map/scatter | solution.py:81
  117.8 26.4 %multiply_reduce_fusion.1 = (f32[6144]{0:T(1024)S(1)}, f32[6144,2048]{1,0:T(8,128)}) fusion(f32[2048]{0:T(1024)} %param.25, f32[2048]{0:T(1024)} %param.24, bf16[6144,256]{1,0:T(8,128)(2,1)S(1)} %scatter_custom_fusion, f32[256,2048]{1,0:T(8,128)} %param.23), kind=kOutput, calls=%fused_computation.35 | convolution fusion | flops 6581381120 | bytes 55615488 | tf_op jit(solution)/shard_map/dot_general | solution.py:83
  144.2 3.6 psum.28
  147.7 23.0 %while.11 = (s32[]{:T(128)}, f32[12,512]{1,0:T(8,128)S(1)}, f32[12,512]{1,0:T(8,128)S(1)}, f32[12,512]{1,0:T(8,128)}, f32[12,512]{1,0:T(8,128)S(1)}, /*index=5*/s32[]{:T(128)}, s32[]{:T(128)}) while((s32[]{:T(128)}, f32[12,512]{1,0:T(8,128)S(1)}, f32[12,512]{1,0:T(8,128)S(1)}, f32[12,512]{1,0:T(8,128)}, f32[12,512]{1,0:T(8,128)S(1)}, ...), condition=%wide.region_5.6_spmd.clone, body=%wide.region_3.5_spmd.clone.sunk | while | flops 4982786 | bytes 32865 | solution.py:34
  148.5 1.1 fusion.43
  150.4 1.1 fusion.43
  152.3 1.1 fusion.43
  154.3 1.1 fusion.43
  156.2 1.1 fusion.43
  158.1 1.1 fusion.43
  160.0 1.1 fusion.43
  161.9 1.1 fusion.43
  163.8 1.1 fusion.43
  167.7 1.1 fusion.43
  169.6 1.1 fusion.43
  170.8 48.6 %fusion.36 = (f32[2048]{0:T(1024)S(1)}, bf16[6144,2048]{1,0:T(8,128)(2,1)}, f32[2048]{0:T(1024)S(1)}) fusion(f32[6144,2048]{1,0:T(8,128)} %get-tuple-element.82, f32[2048]{0:T(1024)S(1)} %copy-done.2, f32[2048]{0:T(1024)S(1)} %copy-done.1, f32[6144]{0:T(1024)S(1)} %div.33), kind=kLoop, calls=%fused_computation.64 | loop fusion | flops 327151616 | bytes 75554816 | tf_op jit(solution)/shard_map/reduce_sum | solution.py:95
  219.5 12.9 %fusion.22 = f32[256,2048]{1,0:T(8,128)} fusion(bf16[6144,256]{1,0:T(8,128)(2,1)S(1)} %scatter_custom_fusion, bf16[6144,2048]{1,0:T(8,128)(2,1)} %get-tuple-element.74), kind=kOutput, calls=%fused_computation.37 | convolution fusion | flops 6442450944 | bytes 30408704 | tf_op jit(solution)/shard_map/dot_general | solution.py:89
  232.4 84.9 %all-reduce = (f32[2048]{0:T(1024)S(1)}, f32[2048]{0:T(1024)S(1)}) all-reduce(f32[2048]{0:T(1024)S(1)} %get-tuple-element.73, f32[2048]{0:T(1024)S(1)} %get-tuple-element.80), channel_id=1, replica_groups=mesh['dp'=16,'mp'=2] {'dp'}, use_global_device_ids=true, to_apply=%region_8.9 | all-reduce | flops 4096 | bytes 32768 | tf_op jit(solution)/shard_map/psum | solution.py:97
  318.0 49.5 %all-reduce.3.cloned.1.call-done = f32[256,2048]{1,0:T(8,128)} async-done(((f32[256,2048]{1,0:T(8,128)}), f32[256,2048]{1,0:T(8,128)}) %all-reduce.3.cloned.1.call-update) | async-done | bytes 2097168 | tf_op jit(solution)/shard_map/psum | solution.py:97
  367.5 7.4 %divide_subtract_fusion = (f32[256,2048]{1,0:T(8,128)}, f32[256,2048]{1,0:T(8,128)}, f32[256,2048]{1,0:T(8,128)}) fusion(f32[256,2048]{1,0:T(8,128)} %param.23, f32[256,2048]{1,0:T(8,128)} %all-reduce.3.cloned.1.call-done, f32[256,2048]{1,0:T(8,128)} %param.26, f32[256,2048]{1,0:T(8,128)} %param.27), kind=kLoop, calls=%fused_computation.41 | loop fusion | flops 5767168 | bytes 14680064 | tf_op jit(solution)/shard_map/sub | solution.py:40
  (87 shorter events, 13.9 us)
Async XLA Ops:
  24.2 64.0 %all-to-all-start.1 = ((bf16[16,384,256]{2,1,0:T(8,128)(2,1)}), bf16[16,384,256]{2,1,0:T(8,128)(2,1)S(1)}, u32[]{:S(2)}, u32[]{:S(2)}) async-start(bf16[16,384,256]{2,1,0:T(8,128)(2,1)} %bitcast.23), calls=%async_computation.1 | async-start | bytes 6291456 | tf_op jit(solution)/shard_map/all_to_all | solution.py:76
  28.0 339.5 %all-reduce.3.cloned.1.call-start = ((), (), s32[]{:S(2)}) async-start(), calls=%async_computation.2 | async-start | bytes 4194304 | tf_op jit(solution)/shard_map/psum | solution.py:97
  88.3 1.7 copy-start
  117.8 53.0 %copy-start.1 = (f32[2048]{0:T(1024)S(1)}, f32[2048]{0:T(1024)}, u32[]{:S(2)}) copy-start(f32[2048]{0:T(1024)} %param.25) | copy-start | bytes 24580
  117.8 53.0 %copy-start.2 = (f32[2048]{0:T(1024)S(1)}, f32[2048]{0:T(1024)}, u32[]{:S(2)}) copy-start(f32[2048]{0:T(1024)} %param.24) | copy-start | bytes 24580
  170.7 48.7 %copy-start.3 = (f32[12,512]{1,0:T(8,128)}, f32[12,512]{1,0:T(8,128)S(1)}, u32[]{:S(2)}) copy-start(f32[12,512]{1,0:T(8,128)S(1)} %get-tuple-element.32) | copy-start | bytes 73732
  219.4 98.0 %copy-start.4 = (f32[2048]{0:T(1024)S(1)}, f32[2048]{0:T(1024)}, u32[]{:S(2)}) copy-start(f32[2048]{0:T(1024)} %param.30) | copy-start | bytes 24580
  219.4 97.9 %copy-start.5 = (f32[2048]{0:T(1024)S(1)}, f32[2048]{0:T(1024)}, u32[]{:S(2)}) copy-start(f32[2048]{0:T(1024)} %param.31) | copy-start | bytes 24580
  219.4 97.9 %copy-start.6 = (f32[2048]{0:T(1024)S(1)}, f32[2048]{0:T(1024)}, u32[]{:S(2)}) copy-start(f32[2048]{0:T(1024)} %param.29) | copy-start | bytes 24580
  219.4 97.9 %copy-start.7 = (f32[2048]{0:T(1024)S(1)}, f32[2048]{0:T(1024)}, u32[]{:S(2)}) copy-start(f32[2048]{0:T(1024)} %param.28) | copy-start | bytes 24580
Sparse Core Ops, SparseCore 0:
  232.5 134.8 all-reduce.2
where the time goes:
time: 383 us; the launch traced here: 382 us
  waiting for transfers between devices  109 us (28%)
  blocking collectives  104 us (27%)
  other arithmetic  71.8 us (19%)
  matrix products  39.3 us (10%)
  local copies, waits for them, and re-layouts  39.2 us (10%)
  between operations  14.2 us (4%)
    psum x1, blocking collectives, per_device(): grad_w, grad_b, grad_o = lax.psum((grad_w, grad_b, grad_o), 'dp')  84.9 us
    all_to_all x1, waiting for transfers between devices, per_device(): lax.all_to_all(blocks, 'dp', split_axis=0, concat_axis=0, tiled=True)  59.5 us
    psum x1, waiting for transfers between devices, per_device(): grad_w, grad_b, grad_o = lax.psum((grad_w, grad_b, grad_o), 'dp')  49.5 us
    reduce_sum x1, other arithmetic, per_device(): grad_b = jnp.sum(grad_pre, axis=0)  48.6 us
    scatter x1, local copies, waits for them, and re-layouts, per_device(): used_rows = jnp.zeros((owner_rows, features), jnp.bfloat16).at[arrived_sl...  27.8 us
    dot_general x1, matrix products, per_device(): jnp.dot(used_rows, w_low, preferred_element_type=jnp.float32) + bias_in  26.4 us
    all_to_all x1, blocking collectives, per_device(): lax.all_to_all(targets, 'dp', split_axis=0, concat_axis=0, tiled=True)  15.5 us
    dot_general x1, matrix products, per_device(): lax.dot_general(used_rows, grad_pre.astype(jnp.bfloat16), (((0,), (0,)),...  12.9 us
  transfers between devices with their start and end apart: 2, of which 2 were waited for; matrix products, arithmetic and copies ran while one was open for 0% of the time, Pallas kernels for 0%

commit v1 on v0

v1 whole, which is shorter than its diff:
```python
import functools
import math

import jax
import jax.numpy as jnp
from jax import lax
from jax.experimental import pallas as pl
from jax.experimental.pallas import tpu as pltpu
from jax.sharding import PartitionSpec as P

beta_one = 0.9
beta_two = 0.95
learn_rate = 0.001
adam_eps = 1e-08

C0 = math.sqrt(2.0 / math.pi)
C1 = C0 * 0.044715
MESH = pl.DeviceIdType.MESH
LANES = 128
BLOCK = 512
BF = jnp.bfloat16
F32 = jnp.float32


def fwd_kernel(x_ref, w_ref, b_ref, wo_ref, h_ref, g_ref, s_ref):
    x = x_ref[...]
    hidden = w_ref.shape[1]
    step = 256
    acc = jnp.zeros((x.shape[0], LANES), F32)
    for c in range(0, hidden, step):
        v = jnp.dot(x, w_ref[:, c : c + step], preferred_element_type=F32) + b_ref[:, c : c + step]
        v2 = v * v
        s = 0.5 * jnp.tanh(v * (C1 * v2 + C0)) + 0.5
        h = v * s
        g = s + (h * (1.0 - s)) * ((6.0 * C1) * v2 + 2.0 * C0)
        hb = h.astype(BF)
        h_ref[:, c : c + step] = hb
        g_ref[:, c : c + step] = g.astype(BF)
        acc = acc + jnp.dot(hb, wo_ref[c : c + step, :], preferred_element_type=F32)
    s_ref[0] = jnp.sum(acc.T, axis=0, keepdims=True)


def forward(rows, w_low, bias, wo_pair):
    total, features = rows.shape
    hidden = w_low.shape[1]
    blocks = total // BLOCK
    return pl.pallas_call(
        fwd_kernel,
        grid=(blocks,),
        in_specs=[
            pl.BlockSpec((BLOCK, features), lambda i: (i, 0)),
            pl.BlockSpec((features, hidden), lambda i: (0, 0)),
            pl.BlockSpec((1, hidden), lambda i: (0, 0)),
            pl.BlockSpec((hidden, LANES), lambda i: (0, 0)),
        ],
        out_specs=[
            pl.BlockSpec((BLOCK, hidden), lambda i: (i, 0)),
            pl.BlockSpec((BLOCK, hidden), lambda i: (i, 0)),
            pl.BlockSpec((1, 1, BLOCK), lambda i: (i, 0, 0)),
        ],
        out_shape=[
            jax.ShapeDtypeStruct((total, hidden), BF),
            jax.ShapeDtypeStruct((total, hidden), BF),
            jax.ShapeDtypeStruct((blocks, 1, BLOCK), F32),
        ],
        compiler_params=pltpu.CompilerParams(vmem_limit_bytes=48 << 20),
    )(rows, w_low, bias, wo_pair)


def split_three(values):
    first = values.astype(BF)
    rest = values - first.astype(F32)
    second = rest.astype(BF)
    third = (rest - second.astype(F32)).astype(BF)
    return first, second, third


def mid_kernel(
    n, scale, msg_ref, gain_ref, keep_ref, weight_ref,
    doc_ref, lam_ref,
    arrive, lam_out, lam_in, s_row, l_row, s_col, g_col, lam_t,
    send_a, recv_a, send_l, recv_l,
):
    me = lax.axis_index("dp")
    core = lax.axis_index("mp")
    other = 1 - core
    high_rows = gain_ref.shape[0]
    per_list = weight_ref.shape[0]
    lists = high_rows // per_list
    cap = msg_ref.shape[2]

    barrier = pltpu.get_barrier_semaphore()

    @pl.loop(1, n)
    def _(k):
        peer = lax.rem(me + k, n)
        pl.semaphore_signal(barrier, inc=1, device_id=(peer, core), device_id_type=MESH)
        pl.semaphore_signal(barrier, inc=1, device_id=(peer, other), device_id_type=MESH)

    pl.semaphore_signal(barrier, inc=1, device_id=(me, other), device_id_type=MESH)
    pl.semaphore_wait(barrier, 2 * n - 1)

    def score_copy(peer, to_core, side):
        return pltpu.make_async_remote_copy(
            src_ref=msg_ref.at[peer],
            dst_ref=arrive.at[core, me],
            send_sem=send_a.at[side, peer],
            recv_sem=recv_a.at[core, me],
            device_id=(peer, to_core),
            device_id_type=MESH,
        )

    def arrival(from_core, peer):
        return pltpu.make_async_remote_copy(
            src_ref=msg_ref.at[peer],
            dst_ref=arrive.at[from_core, peer],
            send_sem=send_a.at[0, peer],
            recv_sem=recv_a.at[from_core, peer],
            device_id=(peer, from_core),
            device_id_type=MESH,
        )

    @pl.loop(1, n)
    def _(k):
        peer = lax.rem(me + k, n)
        score_copy(peer, core, 0).start()
        score_copy(peer, other, 1).start()

    score_copy(me, other, 1).start()
    arrive[core, me] = msg_ref[me]

    high_iota = lax.broadcasted_iota(jnp.int32, (LANES, cap), 0).astype(F32)

    def absorb(shard, total):
        one = arrive[0, shard]
        two = arrive[1, shard]
        value = one[0:1] + two[0:1]
        low = (one[2:3] == high_iota).astype(F32).astype(BF)
        at_high = one[1:2] == high_iota[:high_rows]
        for piece in split_three(value):
            spread = jnp.where(at_high, piece.astype(F32), 0.0).astype(BF)
            total = total + lax.dot_general(
                spread, low, (((1,), (1,)), ((), ())), preferred_element_type=F32
            )
        return total

    arrival(other, me).wait_recv()
    total = absorb(me, jnp.zeros((high_rows, LANES), F32))

    def take(k, total):
        peer = lax.rem(me + k, n)
        arrival(0, peer).wait_recv()
        arrival(1, peer).wait_recv()
        return absorb(peer, total)

    total = lax.fori_loop(1, n, take, total)
    scores = jnp.where(keep_ref[...] > 0.0, 0.5 * total, -1e30)
    s_row[...] = scores
    padding = jnp.zeros((LANES - high_rows, LANES), F32)
    s_turn = jnp.concatenate([scores, padding], axis=0).T
    g_turn = jnp.concatenate([gain_ref[...], padding], axis=0).T
    for i in range(high_rows):
        s_col[i] = s_turn[:, i : i + 1]
        g_col[i] = g_turn[:, i : i + 1]

    def one_list(q, carry):
        base = q * per_list
        row_s = jnp.concatenate([s_row[pl.ds(base + k, 1), :] for k in range(per_list)], axis=1)
        row_g = jnp.concatenate([gain_ref[pl.ds(base + k, 1), :] for k in range(per_list)], axis=1)
        sums = jnp.zeros((8, row_s.shape[1]), F32)
        for k in range(per_list):
            col_s = s_col[base + k]
            col_g = g_col[base + k]
            for r in range(0, LANES, 8):
                delta_g = col_g[r : r + 8] - row_g
                delta_t = jnp.tanh(col_s[r : r + 8] - row_s)
                sums = sums + weight_ref[k, r : r + 8, :] * (delta_g - jnp.abs(delta_g) * delta_t)
        lam = 0.5 * jnp.sum(sums, axis=0, keepdims=True)
        for k in range(per_list):
            l_row[pl.ds(base + k, 1), :] = lam[:, k * LANES : (k + 1) * LANES]
        return carry

    lax.fori_loop(0, lists, one_list, 0)
    doc_ref[...] = l_row[...]
    turned = jnp.concatenate([l_row[...] * scale, padding], axis=0).T
    pieces = split_three(turned)
    for i in range(3):
        lam_t[i] = pieces[i]

    def answer(shard):
        info = arrive[core, shard]
        low = info[2:3] == high_iota
        high = (info[1:2] == high_iota).astype(F32).astype(BF)
        spread = jnp.dot(lam_t[0], high, preferred_element_type=F32)
        spread += jnp.dot(lam_t[1], high, preferred_element_type=F32)
        spread += jnp.dot(lam_t[2], high, preferred_element_type=F32)
        return jnp.sum(jnp.where(low, spread, 0.0), axis=0, keepdims=True)

    def lam_copy(peer):
        return pltpu.make_async_remote_copy(
            src_ref=lam_out.at[peer],
            dst_ref=lam_in.at[me],
            send_sem=send_l.at[peer],
            recv_sem=recv_l.at[me],
            device_id=(peer, core),
            device_id_type=MESH,
        )

    def lam_arrival(peer):
        return pltpu.make_async_remote_copy(
            src_ref=lam_out.at[peer],
            dst_ref=lam_in.at[peer],
            send_sem=send_l.at[peer],
            recv_sem=recv_l.at[peer],
            device_id=(peer, core),
            device_id_type=MESH,
        )

    @pl.loop(1, n)
    def _(k):
        peer = lax.rem(me + k, n)
        lam_out[peer] = answer(peer)
        lam_copy(peer).start()

    lam_ref[me] = answer(me)

    @pl.loop(1, n)
    def _(k):
        peer = lax.rem(me + k, n)
        lam_arrival(peer).wait_recv()
        lam_ref[peer] = lam_in[peer]

    @pl.loop(1, n)
    def _(k):
        peer = lax.rem(me + k, n)
        score_copy(peer, core, 0).wait_send()
        score_copy(peer, other, 1).wait_send()
        lam_copy(peer).wait_send()

    score_copy(me, other, 1).wait_send()


def middle(n, message, gain_rows, keep_rows, weights, query_total):
    cap = message.shape[2]
    high_rows = gain_rows.shape[0]
    vmem = pl.BlockSpec(memory_space=pltpu.VMEM)
    return pl.pallas_call(
        functools.partial(mid_kernel, n, 1.0 / query_total),
        in_specs=[vmem] * 4,
        out_specs=[vmem] * 2,
        out_shape=[
            jax.ShapeDtypeStruct((high_rows, LANES), F32),
            jax.ShapeDtypeStruct((n, 1, cap), F32),
        ],
        scratch_shapes=[
            pltpu.VMEM((2, n, 3, cap), F32),
            pltpu.VMEM((n, 1, cap), F32),
            pltpu.VMEM((n, 1, cap), F32),
            pltpu.VMEM((high_rows, LANES), F32),
            pltpu.VMEM((high_rows, LANES), F32),
            pltpu.VMEM((high_rows, LANES, 1), F32),
            pltpu.VMEM((high_rows, LANES, 1), F32),
            pltpu.VMEM((3, LANES, LANES), BF),
            pltpu.SemaphoreType.DMA((2, n)),
            pltpu.SemaphoreType.DMA((2, n)),
            pltpu.SemaphoreType.DMA((n,)),
            pltpu.SemaphoreType.DMA((n,)),
        ],
        compiler_params=pltpu.CompilerParams(
            collective_id=0, has_side_effects=True, vmem_limit_bytes=48 << 20
        ),
    )(message, gain_rows, keep_rows, weights)


def bwd_kernel(x_ref, h_ref, g_ref, lam_ref, wo_ref, out_ref, acc, acc_o):
    step = pl.program_id(0)
    features = x_ref.shape[1]
    hidden = h_ref.shape[1]
    chunk = 256

    @pl.when(step == 0)
    def _():
        acc[...] = jnp.zeros_like(acc)
        acc_o[...] = jnp.zeros_like(acc_o)

    lam = lam_ref[0]
    top = lam.astype(BF).astype(F32)
    place = lax.broadcasted_iota(jnp.int32, (16, lam.shape[1]), 0)
    pair = jnp.where(place == 0, top, jnp.where(place == 1, lam - top, 0.0)).astype(BF)
    scaled = (x_ref[...].astype(F32).T * lam).astype(BF)
    left = jnp.concatenate([scaled, pair], axis=0)
    for c in range(0, hidden, chunk):
        acc[:, c : c + chunk] += jnp.dot(left, g_ref[:, c : c + chunk], preferred_element_type=F32)
        acc_o[:, c : c + chunk] += jnp.dot(pair, h_ref[:, c : c + chunk], preferred_element_type=F32)

    @pl.when(step == pl.num_programs(0) - 1)
    def _():
        spot = lax.broadcasted_iota(jnp.int32, (16, LANES), 0)
        rest = out_ref.shape[1] - features - 16
        for k in range(hidden // LANES):
            cols = slice(k * LANES, (k + 1) * LANES)
            wo = wo_ref[:, cols]
            out_ref[k, :features, :] = (acc[:features, cols] * wo).astype(BF)
            grad_b = jnp.sum(acc[features:, cols], axis=0, keepdims=True) * wo
            grad_o = jnp.sum(acc_o[:, cols], axis=0, keepdims=True)
            tail = jnp.where(spot == 0, grad_b, jnp.where(spot == 1, grad_o, 0.0))
            out_ref[k, features : features + 16, :] = tail.astype(BF)
            if rest:
                out_ref[k, features + 16 :, :] = jnp.zeros((rest, LANES), BF)


def backward(rows, hid, slope, lam, wo_row, padded):
    total, features = rows.shape
    hidden = hid.shape[1]
    return pl.pallas_call(
        bwd_kernel,
        grid=(total // BLOCK,),
        in_specs=[
            pl.BlockSpec((BLOCK, features), lambda i: (i, 0)),
            pl.BlockSpec((BLOCK, hidden), lambda i: (i, 0)),
            pl.BlockSpec((BLOCK, hidden), lambda i: (i, 0)),
            pl.BlockSpec((1, 1, BLOCK), lambda i: (i, 0, 0)),
            pl.BlockSpec((1, hidden), lambda i: (0, 0)),
        ],
        out_specs=pl.BlockSpec((hidden // LANES, padded, LANES), lambda i: (0, 0, 0)),
        out_shape=jax.ShapeDtypeStruct((hidden // LANES, padded, LANES), BF),
        scratch_shapes=[
            pltpu.VMEM((features + 16, hidden), F32),
            pltpu.VMEM((16, hidden), F32),
        ],
        compiler_params=pltpu.CompilerParams(vmem_limit_bytes=48 << 20),
    )(rows, hid, slope, lam, wo_row)


def sum_kernel(n, in_ref, out_ref, arrive, mine, full, send_a, recv_a, send_b, recv_b):
    me = lax.axis_index("dp")
    core = lax.axis_index("mp")
    barrier = pltpu.get_barrier_semaphore()

    @pl.loop(1, n)
    def _(k):
        peer = lax.rem(me + k, n)
        pl.semaphore_signal(barrier, inc=1, device_id=(peer, core), device_id_type=MESH)

    pl.semaphore_wait(barrier, n - 1)

    def copy(source, target, sends, recvs, peer, slot):
        return pltpu.make_async_remote_copy(
            src_ref=source,
            dst_ref=target.at[slot],
            send_sem=sends.at[peer],
            recv_sem=recvs.at[slot],
            device_id=(peer, core),
            device_id_type=MESH,
        )

    @pl.loop(1, n)
    def _(k):
        peer = lax.rem(me + k, n)
        copy(in_ref.at[peer], arrive, send_a, recv_a, peer, me).start()

    def take(k, total):
        peer = lax.rem(me + n - k, n)
        copy(in_ref.at[peer], arrive, send_a, recv_a, peer, peer).wait_recv()
        return total + arrive[peer].astype(F32)

    total = lax.fori_loop(1, n, take, in_ref[me].astype(F32))
    mine[...] = total.astype(BF)

    @pl.loop(1, n)
    def _(k):
        peer = lax.rem(me + k, n)
        copy(mine, full, send_b, recv_b, peer, me).start()

    out_ref[me] = mine[...]

    @pl.loop(1, n)
    def _(k):
        peer = lax.rem(me + n - k, n)
        copy(mine, full, send_b, recv_b, peer, peer).wait_recv()
        out_ref[peer] = full[peer]

    @pl.loop(1, n)
    def _(k):
        peer = lax.rem(me + k, n)
        copy(in_ref.at[peer], arrive, send_a, recv_a, peer, me).wait_send()
        copy(mine, full, send_b, recv_b, peer, me).wait_send()


def sum_over_dp(n, parts):
    vmem = pl.BlockSpec(memory_space=pltpu.VMEM)
    return pl.pallas_call(
        functools.partial(sum_kernel, n),
        in_specs=[vmem],
        out_specs=vmem,
        out_shape=jax.ShapeDtypeStruct(parts.shape, BF),
        scratch_shapes=[
            pltpu.VMEM(parts.shape, BF),
            pltpu.VMEM(parts.shape[1:], BF),
            pltpu.VMEM(parts.shape, BF),
            pltpu.SemaphoreType.DMA((n,)),
            pltpu.SemaphoreType.DMA((n,)),
            pltpu.SemaphoreType.DMA((n,)),
            pltpu.SemaphoreType.DMA((n,)),
        ],
        compiler_params=pltpu.CompilerParams(
            collective_id=1, has_side_effects=True, vmem_limit_bytes=48 << 20
        ),
    )(parts)


def adam_step(weights, moment, second, gradient):
    moment_next = beta_one * moment + (1.0 - beta_one) * gradient
    second_next = beta_two * second + (1.0 - beta_two) * gradient * gradient
    weights_next = weights - learn_rate * moment_next / (jnp.sqrt(second_next) + adam_eps)
    return (weights_next, moment_next, second_next)


def adam_kernel(g_ref, w_ref, m_ref, s_ref, w_out, m_out, s_out):
    features = w_ref.shape[0]
    for k in range(g_ref.shape[0]):
        cols = slice(k * LANES, (k + 1) * LANES)
        grad = g_ref[k, :features, :].astype(F32)
        w_out[:, cols], m_out[:, cols], s_out[:, cols] = adam_step(
            w_ref[:, cols], m_ref[:, cols], s_ref[:, cols], grad
        )


def adam_matrix(grads, weights, moment, second):
    features, hidden = weights.shape
    group = 4
    block = pl.BlockSpec((features, group * LANES), lambda i: (0, i))
    return pl.pallas_call(
        adam_kernel,
        grid=(hidden // (group * LANES),),
        in_specs=[pl.BlockSpec((group,) + grads.shape[1:], lambda i: (i, 0, 0))] + [block] * 3,
        out_specs=[block] * 3,
        out_shape=[jax.ShapeDtypeStruct(weights.shape, F32)] * 3,
    )(grads, weights, moment, second)


def per_device(
    log_rows, query_ids, doc_ranks, row_counts, list_lengths, gains,
    weight_in, bias_in, weight_out, moment_w, second_w,
    moment_b, second_b, moment_o, second_o,
):
    n = lax.axis_size("dp")
    total, features = log_rows.shape
    cap = total // n
    hidden = weight_in.shape[1]
    list_count, list_width = gains.shape
    high_rows = list_count * list_width // LANES
    per_list = list_width // LANES

    is_live = jnp.arange(cap)[None, :] < row_counts.reshape(n, 1)
    slots = query_ids.reshape(n, cap) % list_count * list_width + doc_ranks.reshape(n, cap)
    high = jnp.where(is_live, slots // LANES, -1).astype(F32)
    low = (slots % LANES).astype(F32)

    positions = jnp.arange(list_width)
    discount = 1.0 / jnp.log2(2.0 + positions.astype(F32))
    weights = jnp.abs(discount[:, None] - discount[None, :]).reshape(per_list, LANES, list_width)
    keep = positions[None, :] < list_lengths[:, None]
    gain_rows = jnp.where(keep, gains, 0.0).reshape(high_rows, LANES)
    keep_rows = keep.astype(F32).reshape(high_rows, LANES)

    wo_top = lax.reduce_precision(weight_out, exponent_bits=8, mantissa_bits=7)
    wo_rest = (weight_out - wo_top).astype(BF)
    wo_top = wo_top.astype(BF)
    lane = jnp.arange(LANES)[None, :]
    wo_pair = jnp.where(
        lane == 0, wo_top[:, None], jnp.where(lane == 1, wo_rest[:, None], jnp.zeros((), BF))
    )

    hid, slope, scores = forward(
        log_rows, weight_in.astype(BF), bias_in.reshape(1, hidden), wo_pair
    )
    message = jnp.stack([scores.reshape(n, cap), high, low], axis=1)
    doc_rows, lam = middle(n, message, gain_rows, keep_rows, weights, list_count * n)
    lambdas = doc_rows.reshape(list_count, list_width)

    spans = hidden // LANES
    row_parts = max(1, n // spans)
    unit = 16 * row_parts
    padded = (features + 16 + unit - 1) // unit * unit
    parts = backward(
        log_rows, hid, slope, lam.reshape(total // BLOCK, 1, BLOCK),
        weight_out.reshape(1, hidden), padded,
    )
    grads = sum_over_dp(n, parts.reshape(n, padded * spans // n, LANES))
    grads = grads.reshape(spans, padded, LANES)
    grad_b = grads[:, features, :].reshape(hidden).astype(F32)
    grad_o = grads[:, features + 1, :].reshape(hidden).astype(F32)
    return (
        lambdas,
        *adam_matrix(grads, weight_in, moment_w, second_w),
        *adam_step(bias_in, moment_b, second_b, grad_b),
        *adam_step(weight_out, moment_o, second_o, grad_o),
    )


def solution(mesh):
    dp, mp, both = P("dp"), P("mp"), P(None, "mp")
    rows = P("dp", None)
    return jax.shard_map(
        per_device,
        mesh=mesh,
        in_specs=(rows, dp, dp, rows, dp, rows, both, mp, mp, both, both, mp, mp, mp, mp),
        out_specs=(rows, both, both, both, mp, mp, mp, mp, mp, mp),
        check_vma=False,
    )
```

time: 383 us -> 156 us (0.41)
  the two profiles are of different devices: /device:TPU:0 before, /device:TPU:31 now
where the time goes in v1:
time: 156 us
  Pallas kernels  147 us (94%)
  other arithmetic  6.16 us (4%)
  local copies, waits for them, and re-layouts  2.08 us (1%)
    pallas_call x1, Pallas kernels, sum_over_dp(): pl.pallas_call(functools.partial(sum_kernel, n), in_specs=[vmem], out_spe...  58 us
    pallas_call x1, Pallas kernels, forward(): pl.pallas_call(fwd_kernel, grid=(blocks,), in_specs=[pl.BlockSpec((BLOCK,...  35.4 us
    pallas_call x1, Pallas kernels, middle(): pl.pallas_call(functools.partial(mid_kernel, n, 1.0 / query_total), in_sp...  25.3 us
    pallas_call x1, Pallas kernels, backward(): pl.pallas_call(bwd_kernel, grid=(total // BLOCK,), in_specs=[pl.BlockSpec...  22 us
    pallas_call x1, Pallas kernels, adam_matrix(): pl.pallas_call(adam_kernel, grid=(hidden // (group * LANES),), in_specs=[...  6.22 us

profile of v1, /device:TPU:31, one launch (start us, length us, event | category | flops | bytes accessed | tf_op | source)
XLA Modules:
  0.0 156.0 jit_solution(17562733246394790119)
XLA Ops:
  0.7 0.9 reduce-precision_convert_fusion
  1.5 0.6 select_select_fusion.wo_ref
  2.1 1.7 %convert_element_type.58.w_ref = bf16[256,2048]{1,0:T(8,128)(2,1)S(1)} convert(f32[256,2048]{1,0:T(8,128)} %w_ref.1) | non-fusion elementwise | flops 524288 | bytes 3145728 | tf_op jit(solution)/shard_map/convert_element_type | solution.py:476
  3.9 0.0 copy-start.6
  3.9 0.0 copy-start.7
  3.9 0.0 copy-start.5
  4.0 35.4 %shard_map.222 = (bf16[6144,2048]{1,0:T(8,128)(2,1)}, bf16[6144,2048]{1,0:T(8,128)(2,1)}, f32[12,1,512]{2,1,0:T(1,128)S(1)}) custom-call(bf16[6144,256]{1,0:T(8,128)(2,1)S(1)} %copy-done, bf16[256,2048]{1,0:T(8,128)(2,1)S(1)} %convert_element_type.58.w_ref, f32[1,2048]{1,0:T(1,128)S(1)} %bitcast.11, bf16[2048,128]{1,0:T(8,128)(2,1)S(1)} %select_select_fusion.wo_ref), custom_call_target="tpu_custom_call" | custom-call | tf_op jit(solution)/shard_map/pallas_call | solution.py:47
  39.4 0.2 fusion.1
  39.6 0.1 pad_maximum_fusion.msg_ref
  39.7 1.1 subtract_abs_fusion.weight_ref
  40.9 0.1 lt.82
  41.0 0.1 lt.83
  41.0 0.1 compare_convert_fusion.keep_ref
  41.1 0.1 fusion
  41.2 1.2 copy-done.2
  42.4 25.3 %shard_map.223 = (f32[48,128]{1,0:T(8,128)S(1)}, f32[16,1,384]{2,1,0:T(1,128)S(1)}) custom-call(f32[16,3,384]{2,1,0:T(4,128)S(1)} %pad_maximum_fusion.msg_ref, f32[48,128]{1,0:T(8,128)S(1)} %reshape.249.gain_ref, f32[48,128]{1,0:T(8,128)S(1)} %compare_convert_fusion.keep_ref, f32[4,128,512]{2,1,0:T(8,128)S(1)} %copy-done.2), custom_call_target="tpu_custom_call" | custom-call | tf_op jit(solution)/shard_map/pallas_call | solution.py:247
  67.7 22.0 %shard_map.224.in_ref = bf16[16,272,128]{2,1,0:T(8,128)(2,1)S(1)} custom-call(bf16[6144,256]{1,0:T(8,128)(2,1)S(1)} %copy-done, bf16[6144,2048]{1,0:T(8,128)(2,1)} %get-tuple-element.20.h_ref, bf16[6144,2048]{1,0:T(8,128)(2,1)} %get-tuple-element.21.g_ref, f32[12,1,512]{2,1,0:T(1,128)S(1)} %bitcast.12, f32[1,2048]{1,0:T(1,128)S(1)} %bitcast.10), custom_call_target="tpu_custom_call" | custom-call | tf_op jit(solution)/shard_map/pallas_call | solution.py:315
  89.7 0.0 copy-start.10
  89.7 0.0 copy-start.11
  89.8 58.0 %shard_map.225.g_ref = bf16[16,272,128]{2,1,0:T(8,128)(2,1)S(1)} custom-call(bf16[16,272,128]{2,1,0:T(8,128)(2,1)S(1)} %shard_map.224.in_ref), custom_call_target="tpu_custom_call" | custom-call | tf_op jit(solution)/shard_map/pallas_call | solution.py:392
  147.8 0.7 divide_subtract_fusion
  148.6 0.6 divide_subtract_fusion.1
  149.2 6.2 %shard_map.226 = (f32[256,2048]{1,0:T(8,128)}, f32[256,2048]{1,0:T(8,128)}, f32[256,2048]{1,0:T(8,128)}) custom-call(bf16[16,272,128]{2,1,0:T(8,128)(2,1)} %copy-done.1, f32[256,2048]{1,0:T(8,128)} %w_ref.1, f32[256,2048]{1,0:T(8,128)} %m_ref.1, f32[256,2048]{1,0:T(8,128)} %s_ref.1), custom_call_target="tpu_custom_call" | custom-call | tf_op jit(solution)/shard_map/pallas_call | solution.py:433
  155.4 0.6 reshape.250
  (31 shorter events, 0.2 us)
Async XLA Ops:
  0.6 3.2 %copy-start.4 = (f32[2048]{0:T(1024)S(1)}, f32[2048]{0:T(1024)}, u32[]{:S(2)}) copy-start(f32[2048]{0:T(1024)} %param.22) | copy-start | bytes 24580
  0.7 3.2 %copy-start = (bf16[6144,256]{1,0:T(8,128)(2,1)S(1)}, bf16[6144,256]{1,0:T(8,128)(2,1)}, u32[]{:S(2)}) copy-start(bf16[6144,256]{1,0:T(8,128)(2,1)} %x_ref.3) | copy-start | bytes 9437188
  3.9 35.5 %copy-start.6 = (s32[6144]{0:T(1024)S(1)}, s32[6144]{0:T(1024)}, u32[]{:S(2)}) copy-start(s32[6144]{0:T(1024)} %param.16) | copy-start | bytes 73732
  3.9 35.5 %copy-start.7 = (s32[6144]{0:T(1024)S(1)}, s32[6144]{0:T(1024)}, u32[]{:S(2)}) copy-start(s32[6144]{0:T(1024)} %param.17) | copy-start | bytes 73732
  3.9 35.5 %copy-start.13 = (s32[1,16]{1,0:T(1,128)S(1)}, s32[1,16]{1,0:T(1,128)}, u32[]{:S(2)}) copy-start(s32[1,16]{1,0:T(1,128)} %param.18) | copy-start | bytes 196
  3.9 37.0 %copy-start.12 = (s32[12]{0:T(128)S(1)}, s32[12]{0:T(128)}, u32[]{:S(2)}) copy-start(s32[12]{0:T(128)} %param.19) | copy-start | bytes 148
  3.9 37.2 %copy-start.5 = (f32[12,512]{1,0:T(8,128)S(1)}, f32[12,512]{1,0:T(8,128)}, u32[]{:S(2)}) copy-start(f32[12,512]{1,0:T(8,128)} %param.20) | copy-start | bytes 73732
  39.4 28.3 %copy-start.3 = (f32[2048]{0:T(1024)S(1)}, f32[2048]{0:T(1024)}, u32[]{:S(2)}) copy-start(f32[2048]{0:T(1024)} %param.23) | copy-start | bytes 24580
  41.2 1.2 copy-start.2
  89.7 58.1 %copy-start.8 = (f32[2048]{0:T(1024)S(1)}, f32[2048]{0:T(1024)}, u32[]{:S(2)}) copy-start(f32[2048]{0:T(1024)} %param.28) | copy-start | bytes 24580
  89.7 58.1 %copy-start.9 = (f32[2048]{0:T(1024)S(1)}, f32[2048]{0:T(1024)}, u32[]{:S(2)}) copy-start(f32[2048]{0:T(1024)} %param.29) | copy-start | bytes 24580
  89.7 58.8 %copy-start.10 = (f32[2048]{0:T(1024)S(1)}, f32[2048]{0:T(1024)}, u32[]{:S(2)}) copy-start(f32[2048]{0:T(1024)} %param.26) | copy-start | bytes 24580
  89.7 58.8 %copy-start.11 = (f32[2048]{0:T(1024)S(1)}, f32[2048]{0:T(1024)}, u32[]{:S(2)}) copy-start(f32[2048]{0:T(1024)} %param.27) | copy-start | bytes 24580
  147.8 1.4 copy-start.1

commit v2 on v1

v2 whole, which is shorter than its diff:
```python
import functools
import math

import jax
import jax.numpy as jnp
from jax import lax
from jax.experimental import pallas as pl
from jax.experimental.pallas import tpu as pltpu
from jax.sharding import PartitionSpec as P

beta_one = 0.9
beta_two = 0.95
learn_rate = 0.001
adam_eps = 1e-08

C0 = math.sqrt(2.0 / math.pi)
C1 = C0 * 0.044715
MESH = pl.DeviceIdType.MESH
LANES = 128
BLOCK = 512
WIDE = 256
BF = jnp.bfloat16
F32 = jnp.float32


def fwd_kernel(x_ref, w_ref, b_ref, wo_ref, h_ref, g_ref, s_ref, w_low):
    @pl.when(pl.program_id(0) == 0)
    def _():
        w_low[...] = w_ref[...].astype(BF)

    x = x_ref[...]
    acc = jnp.zeros((x.shape[0], LANES), F32)
    for k in range(h_ref.shape[0]):
        cols = slice(k * WIDE, (k + 1) * WIDE)
        v = jnp.dot(x, w_low[:, cols], preferred_element_type=F32) + b_ref[:, cols]
        v2 = v * v
        t = jnp.tanh(v * (C1 * v2 + C0))
        up = 1.0 + t
        h = v * up
        g = up + (h * (1.0 - t)) * ((3.0 * C1) * v2 + C0)
        hb = h.astype(BF)
        h_ref[k] = hb
        g_ref[k] = g.astype(BF)
        acc = acc + jnp.dot(hb, wo_ref[cols, :], preferred_element_type=F32)
    s_ref[0] = jnp.sum(acc.T, axis=0, keepdims=True)


def forward(rows, weights, bias, wo_pair):
    total, features = rows.shape
    hidden = weights.shape[1]
    blocks = total // BLOCK
    groups = hidden // WIDE
    return pl.pallas_call(
        fwd_kernel,
        grid=(blocks,),
        in_specs=[
            pl.BlockSpec((BLOCK, features), lambda i: (i, 0)),
            pl.BlockSpec((features, hidden), lambda i: (0, 0)),
            pl.BlockSpec((1, hidden), lambda i: (0, 0)),
            pl.BlockSpec((hidden, LANES), lambda i: (0, 0)),
        ],
        out_specs=[
            pl.BlockSpec((groups, BLOCK, WIDE), lambda i: (0, i, 0)),
            pl.BlockSpec((groups, BLOCK, WIDE), lambda i: (0, i, 0)),
            pl.BlockSpec((1, 1, BLOCK), lambda i: (i, 0, 0)),
        ],
        out_shape=[
            jax.ShapeDtypeStruct((groups, total, WIDE), BF),
            jax.ShapeDtypeStruct((groups, total, WIDE), BF),
            jax.ShapeDtypeStruct((blocks, 1, BLOCK), F32),
        ],
        scratch_shapes=[pltpu.VMEM((features, hidden), BF)],
        compiler_params=pltpu.CompilerParams(vmem_limit_bytes=48 << 20),
    )(rows, weights, bias, wo_pair)


def split_three(values):
    first = values.astype(BF)
    rest = values - first.astype(F32)
    second = rest.astype(BF)
    third = (rest - second.astype(F32)).astype(BF)
    return first, second, third


def mid_kernel(
    n, cores, scale, msg_ref, gain_ref, keep_ref, weight_ref,
    doc_ref, lam_ref,
    arrive, lam_out, lam_in, s_row, l_row, s_col, g_col, lam_t,
    send_a, recv_a, send_l, recv_l,
):
    me = lax.axis_index("dp")
    core = lax.axis_index("mp")
    high_rows = gain_ref.shape[0]
    per_list = weight_ref.shape[0]
    lists = high_rows // per_list
    cap = msg_ref.shape[2]

    barrier = pltpu.get_barrier_semaphore()

    @pl.loop(1, n)
    def _(k):
        peer = lax.rem(me + k, n)
        for d in range(cores):
            pl.semaphore_signal(
                barrier, inc=1, device_id=(peer, lax.rem(core + d, cores)), device_id_type=MESH
            )

    for d in range(1, cores):
        pl.semaphore_signal(
            barrier, inc=1, device_id=(me, lax.rem(core + d, cores)), device_id_type=MESH
        )
    pl.semaphore_wait(barrier, cores * n - 1)

    def score_copy(peer, d):
        return pltpu.make_async_remote_copy(
            src_ref=msg_ref.at[peer],
            dst_ref=arrive.at[core, me],
            send_sem=send_a.at[d, peer],
            recv_sem=recv_a.at[core, me],
            device_id=(peer, lax.rem(core + d, cores)),
            device_id_type=MESH,
        )

    def arrival(from_core, peer):
        return pltpu.make_async_remote_copy(
            src_ref=msg_ref.at[peer],
            dst_ref=arrive.at[from_core, peer],
            send_sem=send_a.at[0, peer],
            recv_sem=recv_a.at[from_core, peer],
            device_id=(peer, from_core),
            device_id_type=MESH,
        )

    @pl.loop(1, n)
    def _(k):
        peer = lax.rem(me + k, n)
        for d in range(cores):
            score_copy(peer, d).start()

    for d in range(1, cores):
        score_copy(me, d).start()
    arrive[core, me] = msg_ref[me]

    high_iota = lax.broadcasted_iota(jnp.int32, (LANES, cap), 0).astype(F32)

    def absorb(shard, total):
        first = arrive[0, shard]
        value = first[0:1]
        for c in range(1, cores):
            value = value + arrive[c, shard][0:1]
        low = (first[2:3] == high_iota).astype(F32).astype(BF)
        at_high = first[1:2] == high_iota[:high_rows]
        spread = jnp.concatenate(
            [jnp.where(at_high, piece.astype(F32), 0.0).astype(BF) for piece in split_three(value)],
            axis=0,
        )
        sums = lax.dot_general(
            spread, low, (((1,), (1,)), ((), ())), preferred_element_type=F32
        )
        return total + (
            sums[:high_rows] + sums[high_rows : 2 * high_rows] + sums[2 * high_rows :]
        )

    for d in range(1, cores):
        arrival(lax.rem(core + d, cores), me).wait_recv()
    total = absorb(me, jnp.zeros((high_rows, LANES), F32))

    def take(k, total):
        for j in range(3):
            for c in range(cores):
                arrival(c, lax.rem(me + 1 + 3 * k + j, n)).wait_recv()
        for j in range(3):
            total = absorb(lax.rem(me + 1 + 3 * k + j, n), total)
        return total

    total = lax.fori_loop(0, (n - 1) // 3, take, total)
    scores = jnp.where(keep_ref[...] > 0.0, 0.5 * total, -1e30)
    s_row[...] = scores
    padding = jnp.zeros((LANES - high_rows, LANES), F32)
    s_turn = jnp.concatenate([scores, padding], axis=0).T
    g_turn = jnp.concatenate([gain_ref[...], padding], axis=0).T
    for i in range(high_rows):
        s_col[i] = s_turn[:, i : i + 1]
        g_col[i] = g_turn[:, i : i + 1]

    def one_list(q, carry):
        base = q * per_list
        row_s = jnp.concatenate([s_row[pl.ds(base + k, 1), :] for k in range(per_list)], axis=1)
        row_g = jnp.concatenate([gain_ref[pl.ds(base + k, 1), :] for k in range(per_list)], axis=1)
        sums = jnp.zeros((8, row_s.shape[1]), F32)
        for k in range(per_list):
            col_s = s_col[base + k]
            col_g = g_col[base + k]
            for r in range(0, LANES, 8):
                delta_g = col_g[r : r + 8] - row_g
                delta_t = jnp.tanh(col_s[r : r + 8] - row_s)
                sums = sums + weight_ref[k, r : r + 8, :] * (delta_g - jnp.abs(delta_g) * delta_t)
        lam = 0.5 * jnp.sum(sums, axis=0, keepdims=True)
        for k in range(per_list):
            l_row[pl.ds(base + k, 1), :] = lam[:, k * LANES : (k + 1) * LANES]
        return carry

    lax.fori_loop(0, lists, one_list, 0)
    doc_ref[...] = l_row[...]
    turned = jnp.concatenate([l_row[...] * scale, padding], axis=0).T
    lam_t[...] = jnp.concatenate(split_three(turned), axis=1)

    def answer(shard):
        info = arrive[core, shard]
        low = info[2:3] == high_iota
        high = (info[1:2] == high_iota).astype(F32).astype(BF)
        spread = jnp.dot(
            lam_t[...], jnp.concatenate([high] * 3, axis=0), preferred_element_type=F32
        )
        return jnp.sum(jnp.where(low, spread, 0.0), axis=0, keepdims=True)

    def lam_copy(peer):
        return pltpu.make_async_remote_copy(
            src_ref=lam_out.at[peer],
            dst_ref=lam_in.at[me],
            send_sem=send_l.at[peer],
            recv_sem=recv_l.at[me],
            device_id=(peer, core),
            device_id_type=MESH,
        )

    def lam_arrival(peer):
        return pltpu.make_async_remote_copy(
            src_ref=lam_out.at[peer],
            dst_ref=lam_in.at[peer],
            send_sem=send_l.at[peer],
            recv_sem=recv_l.at[peer],
            device_id=(peer, core),
            device_id_type=MESH,
        )

    @pl.loop(0, (n - 1) // 3)
    def _(k):
        peers = [lax.rem(me + 1 + 3 * k + j, n) for j in range(3)]
        replies = [answer(peer) for peer in peers]
        for peer, reply in zip(peers, replies):
            lam_out[peer] = reply
        for peer in peers:
            lam_copy(peer).start()

    lam_ref[me] = answer(me)

    @pl.loop(1, n)
    def _(k):
        peer = lax.rem(me + k, n)
        lam_arrival(peer).wait_recv()
        lam_ref[peer] = lam_in[peer]

    @pl.loop(1, n)
    def _(k):
        peer = lax.rem(me + k, n)
        for d in range(cores):
            score_copy(peer, d).wait_send()
        lam_copy(peer).wait_send()

    for d in range(1, cores):
        score_copy(me, d).wait_send()


def middle(n, cores, message, gain_rows, keep_rows, weights, query_total):
    cap = message.shape[2]
    high_rows = gain_rows.shape[0]
    vmem = pl.BlockSpec(memory_space=pltpu.VMEM)
    return pl.pallas_call(
        functools.partial(mid_kernel, n, cores, 1.0 / query_total),
        in_specs=[vmem] * 4,
        out_specs=[vmem] * 2,
        out_shape=[
            jax.ShapeDtypeStruct((high_rows, LANES), F32),
            jax.ShapeDtypeStruct((n, 1, cap), F32),
        ],
        scratch_shapes=[
            pltpu.VMEM((cores, n, 3, cap), F32),
            pltpu.VMEM((n, 1, cap), F32),
            pltpu.VMEM((n, 1, cap), F32),
            pltpu.VMEM((high_rows, LANES), F32),
            pltpu.VMEM((high_rows, LANES), F32),
            pltpu.VMEM((high_rows, LANES, 1), F32),
            pltpu.VMEM((high_rows, LANES, 1), F32),
            pltpu.VMEM((LANES, 3 * LANES), BF),
            pltpu.SemaphoreType.DMA((cores, n)),
            pltpu.SemaphoreType.DMA((cores, n)),
            pltpu.SemaphoreType.DMA((n,)),
            pltpu.SemaphoreType.DMA((n,)),
        ],
        compiler_params=pltpu.CompilerParams(
            collective_id=0, has_side_effects=True, vmem_limit_bytes=48 << 20
        ),
    )(message, gain_rows, keep_rows, weights)


def tail_rows(grad_b, grad_o):
    spot = lax.broadcasted_iota(jnp.int32, (16, grad_b.shape[1]), 0)
    top_b = grad_b.astype(BF).astype(F32)
    top_o = grad_o.astype(BF).astype(F32)
    tail = jnp.where(spot == 0, top_b, jnp.where(spot == 1, top_o, 0.0))
    tail = jnp.where(spot == 2, grad_b - top_b, jnp.where(spot == 3, grad_o - top_o, tail))
    return tail.astype(BF)


def grad_kernel(
    n, parts_per_span, x_ref, lam_ref, wo_ref, h_hbm, g_hbm, out_ref,
    left, h_buf, g_buf, parts, arrive, mine, full,
    fetch_sem, send_a, recv_a, send_b, recv_b,
):
    me = lax.axis_index("dp")
    core = lax.axis_index("mp")
    groups = h_hbm.shape[0]
    features = x_ref.shape[1]
    chunk_rows = parts.shape[1]
    padded = chunk_rows * parts_per_span
    per_group = WIDE // LANES * parts_per_span
    first = me // per_group + 1

    def fetches(k):
        group = lax.rem(first + k, groups)
        slot = lax.rem(k, 2)
        return (
            pltpu.make_async_copy(g_hbm.at[group], g_buf.at[slot], fetch_sem.at[slot, 0]),
            pltpu.make_async_copy(h_hbm.at[group], h_buf.at[slot], fetch_sem.at[slot, 1]),
        )

    for one in fetches(0):
        one.start()

    barrier = pltpu.get_barrier_semaphore()

    @pl.loop(1, n)
    def _(k):
        peer = lax.rem(me + k, n)
        pl.semaphore_signal(barrier, inc=1, device_id=(peer, core), device_id_type=MESH)

    @pl.loop(0, lam_ref.shape[0])
    def _(i):
        lam = lam_ref[i]
        top = lam.astype(BF).astype(F32)
        place = lax.broadcasted_iota(jnp.int32, (16, BLOCK), 0)
        pair = jnp.where(place == 0, top, jnp.where(place == 1, lam - top, 0.0)).astype(BF)
        at = pl.ds(pl.multiple_of(i * BLOCK, BLOCK), BLOCK)
        left[:features, at] = (x_ref[at, :].astype(F32).T * lam).astype(BF)
        left[features:, at] = pair

    pl.semaphore_wait(barrier, n - 1)

    def copy(source, target, send, recvs, peer, slot):
        return pltpu.make_async_remote_copy(
            src_ref=source,
            dst_ref=target.at[slot],
            send_sem=send,
            recv_sem=recvs.at[slot],
            device_id=(peer, core),
            device_id_type=MESH,
        )

    @pl.loop(0, groups)
    def _(k):
        for one in fetches(k):
            one.wait()

        @pl.when(k + 1 < groups)
        def _():
            for one in fetches(k + 1):
                one.start()

        group = lax.rem(first + k, groups)
        slot = lax.rem(k, 2)
        half_wo = wo_ref[group]
        sums = jnp.dot(left[...], g_buf[slot], preferred_element_type=F32)
        sums_o = jnp.dot(left[features:, :], h_buf[slot], preferred_element_type=F32)
        grad_b = jnp.sum(sums[features:], axis=0, keepdims=True) * half_wo
        grad_o = 0.5 * jnp.sum(sums_o, axis=0, keepdims=True)
        pieces = [
            (sums[:features] * half_wo).astype(BF),
            tail_rows(grad_b, grad_o),
        ]
        if padded > features + 16:
            pieces.append(jnp.zeros((padded - features - 16, WIDE), BF))
        block = jnp.concatenate(pieces, axis=0)
        for j in range(per_group):
            span, part = j // parts_per_span, j % parts_per_span
            parts[group * per_group + j] = block[
                part * chunk_rows : (part + 1) * chunk_rows, span * LANES : (span + 1) * LANES
            ]
        for j in range(per_group):
            owner = group * per_group + j

            @pl.when(owner != me)
            def _():
                copy(parts.at[owner], arrive, send_a.at[owner], recv_a, owner, me).start()

    def take(k, total):
        peer = lax.rem(me + n - k, n)
        copy(parts.at[peer], arrive, send_a.at[peer], recv_a, peer, peer).wait_recv()
        return total + arrive[peer].astype(F32)

    total = lax.fori_loop(1, n, take, parts[me].astype(F32))
    mine[...] = total.astype(BF)

    @pl.when(lax.rem(me, parts_per_span) == features // chunk_rows)
    def _():
        at = features % chunk_rows
        mine[at : at + 16, :] = tail_rows(
            total[at : at + 1] + total[at + 2 : at + 3],
            total[at + 1 : at + 2] + total[at + 3 : at + 4],
        )

    inner = 4
    outer = n // inner
    row, col = me // inner, lax.rem(me, inner)

    def outer_peer(i):
        return lax.rem(row + i, outer) * inner + col

    def inner_peer(j):
        return row * inner + lax.rem(col + j, inner)

    def send_outer(i):
        peer = outer_peer(i)
        return copy(mine, full, send_b.at[0, peer], recv_b, peer, me)

    def send_inner(j):
        return copy(mine, full, send_b.at[j, me], recv_b, inner_peer(j), me)

    def pass_on(i, j):
        chunk = outer_peer(outer - i)
        return copy(full.at[chunk], full, send_b.at[j, chunk], recv_b, inner_peer(j), chunk)

    def landed(chunk):
        return copy(mine, full, send_b.at[0, chunk], recv_b, me, chunk)

    for i in range(1, outer):
        send_outer(i).start()
    for j in range(1, inner):
        send_inner(j).start()
    out_ref[me] = mine[...]
    for i in range(1, outer):
        chunk = outer_peer(outer - i)
        landed(chunk).wait_recv()
        for j in range(1, inner):
            pass_on(i, j).start()
        out_ref[chunk] = full[chunk]
    for i in range(outer):
        for j in range(1, inner):
            chunk = lax.rem(row + outer - i, outer) * inner + lax.rem(col + j, inner)
            landed(chunk).wait_recv()
            out_ref[chunk] = full[chunk]

    @pl.loop(1, n)
    def _(k):
        peer = lax.rem(me + k, n)
        copy(parts.at[peer], arrive, send_a.at[peer], recv_a, peer, me).wait_send()

    for i in range(1, outer):
        send_outer(i).wait_send()
        for j in range(1, inner):
            pass_on(i, j).wait_send()
    for j in range(1, inner):
        send_inner(j).wait_send()


def gradients(n, rows, hid, slope, lam, wo_half, parts_per_span, chunk_rows):
    total, features = rows.shape
    groups = hid.shape[0]
    vmem = pl.BlockSpec(memory_space=pltpu.VMEM)
    hbm = pl.BlockSpec(memory_space=pl.ANY)
    shape = (n, chunk_rows, LANES)
    return pl.pallas_call(
        functools.partial(grad_kernel, n, parts_per_span),
        in_specs=[vmem, vmem, vmem, hbm, hbm],
        out_specs=vmem,
        out_shape=jax.ShapeDtypeStruct(shape, BF),
        scratch_shapes=[
            pltpu.VMEM((features + 16, total), BF),
            pltpu.VMEM((2, total, WIDE), BF),
            pltpu.VMEM((2, total, WIDE), BF),
            pltpu.VMEM(shape, BF),
            pltpu.VMEM(shape, BF),
            pltpu.VMEM(shape[1:], BF),
            pltpu.VMEM(shape, BF),
            pltpu.SemaphoreType.DMA((2, 2)),
            pltpu.SemaphoreType.DMA((n,)),
            pltpu.SemaphoreType.DMA((n,)),
            pltpu.SemaphoreType.DMA((4, n)),
            pltpu.SemaphoreType.DMA((n,)),
        ],
        compiler_params=pltpu.CompilerParams(
            collective_id=1, has_side_effects=True, vmem_limit_bytes=48 << 20
        ),
    )(rows, lam, wo_half, hid, slope)


def adam_step(weights, moment, second, gradient):
    moment_next = beta_one * moment + (1.0 - beta_one) * gradient
    second_next = beta_two * second + (1.0 - beta_two) * gradient * gradient
    weights_next = weights - learn_rate * moment_next / (jnp.sqrt(second_next) + adam_eps)
    return (weights_next, moment_next, second_next)


def adam_kernel(g_ref, w_ref, m_ref, s_ref, w_out, m_out, s_out):
    features = w_ref.shape[0]
    for k in range(g_ref.shape[0]):
        cols = slice(k * LANES, (k + 1) * LANES)
        grad = g_ref[k, :features, :].astype(F32)
        w_out[:, cols], m_out[:, cols], s_out[:, cols] = adam_step(
            w_ref[:, cols], m_ref[:, cols], s_ref[:, cols], grad
        )


def adam_matrix(grads, weights, moment, second):
    features, hidden = weights.shape
    group = 4
    block = pl.BlockSpec((features, group * LANES), lambda i: (0, i))
    return pl.pallas_call(
        adam_kernel,
        grid=(hidden // (group * LANES),),
        in_specs=[pl.BlockSpec((group,) + grads.shape[1:], lambda i: (i, 0, 0))] + [block] * 3,
        out_specs=[block] * 3,
        out_shape=[jax.ShapeDtypeStruct(weights.shape, F32)] * 3,
    )(grads, weights, moment, second)


def per_device(
    log_rows, query_ids, doc_ranks, row_counts, list_lengths, gains,
    weight_in, bias_in, weight_out, moment_w, second_w,
    moment_b, second_b, moment_o, second_o,
):
    n = lax.axis_size("dp")
    total, features = log_rows.shape
    cap = total // n
    hidden = weight_in.shape[1]
    list_count, list_width = gains.shape
    high_rows = list_count * list_width // LANES
    per_list = list_width // LANES

    is_live = jnp.arange(cap)[None, :] < row_counts.reshape(n, 1)
    slots = query_ids.reshape(n, cap) % list_count * list_width + doc_ranks.reshape(n, cap)
    high = jnp.where(is_live, slots // LANES, -1).astype(F32)
    low = (slots % LANES).astype(F32)

    positions = jnp.arange(list_width)
    discount = 1.0 / jnp.log2(2.0 + positions.astype(F32))
    weights = jnp.abs(discount[:, None] - discount[None, :]).reshape(per_list, LANES, list_width)
    keep = positions[None, :] < list_lengths[:, None]
    gain_rows = jnp.where(keep, gains, 0.0).reshape(high_rows, LANES)
    keep_rows = keep.astype(F32).reshape(high_rows, LANES)

    wo_half = 0.5 * weight_out
    wo_top = lax.reduce_precision(wo_half, exponent_bits=8, mantissa_bits=7)
    wo_rest = (wo_half - wo_top).astype(BF)
    wo_top = wo_top.astype(BF)
    lane = jnp.arange(LANES)[None, :]
    wo_pair = jnp.where(
        lane == 0, wo_top[:, None], jnp.where(lane == 1, wo_rest[:, None], jnp.zeros((), BF))
    )

    hid, slope, scores = forward(log_rows, weight_in, bias_in.reshape(1, hidden), wo_pair)
    message = jnp.stack([scores.reshape(n, cap), high, low], axis=1)
    doc_rows, lam = middle(
        n, lax.axis_size("mp"), message, gain_rows, keep_rows, weights, list_count * n
    )
    lambdas = doc_rows.reshape(list_count, list_width)

    spans = hidden // LANES
    row_parts = max(1, n // spans)
    unit = 16 * row_parts
    padded = (features + 16 + unit - 1) // unit * unit
    grads = gradients(
        n, log_rows, hid, slope, lam.reshape(total // BLOCK, 1, BLOCK),
        wo_half.reshape(hidden // WIDE, 1, WIDE), row_parts, padded // row_parts,
    )
    grads = grads.reshape(spans, padded, LANES)
    tail = grads[:, features : features + 4, :].astype(F32)
    grad_b = (tail[:, 0] + tail[:, 2]).reshape(hidden)
    grad_o = (tail[:, 1] + tail[:, 3]).reshape(hidden)
    return (
        lambdas,
        *adam_matrix(grads, weight_in, moment_w, second_w),
        *adam_step(bias_in, moment_b, second_b, grad_b),
        *adam_step(weight_out, moment_o, second_o, grad_o),
    )


def solution(mesh):
    dp, mp, both = P("dp"), P("mp"), P(None, "mp")
    rows = P("dp", None)
    return jax.shard_map(
        per_device,
        mesh=mesh,
        in_specs=(rows, dp, dp, rows, dp, rows, both, mp, mp, both, both, mp, mp, mp, mp),
        out_specs=(rows, both, both, both, mp, mp, mp, mp, mp, mp),
        check_vma=False,
    )
```

time: 156 us -> 132 us (0.85)
  the two profiles are of different devices: /device:TPU:31 before, /device:TPU:0 now
where the time goes in v2:
time: 132 us; the launch traced here: 131 us
  Pallas kernels  119 us (90%)
  local copies, waits for them, and re-layouts  7.26 us (6%)
  other arithmetic  4.19 us (3%)
    pallas_call x1, Pallas kernels, gradients(): pl.pallas_call(functools.partial(grad_kernel, n, parts_per_span), in_spec...  51.3 us
    pallas_call x1, Pallas kernels, forward(): pl.pallas_call(fwd_kernel, grid=(blocks,), in_specs=[pl.BlockSpec((BLOCK,...  34.2 us
    pallas_call x1, Pallas kernels, middle(): pl.pallas_call(functools.partial(mid_kernel, n, cores, 1.0 / query_total)...  27.1 us
    unnamed x34, local copies, waits for them, and re-layouts  6.47 us
    pallas_call x1, Pallas kernels, adam_matrix(): pl.pallas_call(adam_kernel, grid=(hidden // (group * LANES),), in_specs=[...  6.21 us

profile of v2, /device:TPU:0, one launch (start us, length us, event | category | flops | bytes accessed | tf_op | source)
XLA Modules:
  0.0 131.2 jit_solution(9261591895395261546)
XLA Ops:
  0.6 0.7 broadcast_multiply_fusion
  1.4 0.6 select_select_fusion.wo_ref
  2.0 0.0 copy-start
  2.0 1.9 %copy-done = bf16[6144,256]{1,0:T(8,128)(2,1)S(1)} copy-done((bf16[6144,256]{1,0:T(8,128)(2,1)S(1)}, bf16[6144,256]{1,0:T(8,128)(2,1)}, u32[]{:S(2)}) %copy-start) | copy-done | bytes 3145752
  3.9 1.6 %copy-done.2 = f32[256,2048]{1,0:T(8,128)S(1)} copy-done((f32[256,2048]{1,0:T(8,128)S(1)}, f32[256,2048]{1,0:T(8,128)}, u32[]{:S(2)}) %copy-start.2) | copy-done | bytes 2097176
  5.5 0.7 copy-done.5
  6.2 0.0 copy-start.8
  6.2 34.2 %shard_map.222 = (bf16[8,6144,256]{2,1,0:T(8,128)(2,1)}, bf16[8,6144,256]{2,1,0:T(8,128)(2,1)}, f32[12,1,512]{2,1,0:T(1,128)S(1)}) custom-call(bf16[6144,256]{1,0:T(8,128)(2,1)S(1)} %copy-done, f32[256,2048]{1,0:T(8,128)S(1)} %copy-done.2, f32[1,2048]{1,0:T(1,128)S(1)} %bitcast.10, bf16[2048,128]{1,0:T(8,128)(2,1)S(1)} %select_select_fusion.wo_ref), custom_call_target="tpu_custom_call" | custom-call | tf_op jit(solution)/shard_map/pallas_call | solution.py:53
  40.4 0.2 fusion.1
  40.7 0.1 pad_maximum_fusion.msg_ref
  40.8 1.1 subtract_abs_fusion.weight_ref
  41.9 0.1 lt.82
  42.0 0.1 lt.83
  42.1 0.1 compare_convert_fusion.keep_ref
  42.1 0.1 fusion
  42.2 1.2 copy-done.4
  43.5 27.1 %shard_map.223 = (f32[48,128]{1,0:T(8,128)S(1)}, f32[16,1,384]{2,1,0:T(1,128)S(1)}) custom-call(f32[16,3,384]{2,1,0:T(4,128)S(1)} %pad_maximum_fusion.msg_ref, f32[48,128]{1,0:T(8,128)S(1)} %reshape.253.gain_ref, f32[48,128]{1,0:T(8,128)S(1)} %compare_convert_fusion.keep_ref, f32[4,128,512]{2,1,0:T(8,128)S(1)} %copy-done.4), custom_call_target="tpu_custom_call" | custom-call | tf_op jit(solution)/shard_map/pallas_call | solution.py:269
  70.6 0.0 copy-start.11
  70.7 51.3 %shard_map.224.g_ref = bf16[16,272,128]{2,1,0:T(8,128)(2,1)S(1)} custom-call(bf16[6144,256]{1,0:T(8,128)(2,1)S(1)} %copy-done.1, f32[12,1,512]{2,1,0:T(1,128)S(1)} %bitcast.12, f32[8,1,256]{2,1,0:T(1,128)S(1)} %bitcast.11, bf16[8,6144,256]{2,1,0:T(8,128)(2,1)} %get-tuple-element.21.h_hbm, bf16[8,6144,256]{2,1,0:T(8,128)(2,1)} %get-tuple-element.22.g_hbm), custom_call_target="tpu_custom_call" | custom-call | tf_op jit(solution)/shard_map/pallas_call | solution.py:472
  122.0 1.0 copy-done.3
  123.1 0.6 divide_subtract_fusion
  123.7 0.6 divide_subtract_fusion.1
  124.3 6.2 %shard_map.225 = (f32[256,2048]{1,0:T(8,128)}, f32[256,2048]{1,0:T(8,128)}, f32[256,2048]{1,0:T(8,128)}) custom-call(bf16[16,272,128]{2,1,0:T(8,128)(2,1)} %copy-done.3, f32[256,2048]{1,0:T(8,128)} %w_ref.3, f32[256,2048]{1,0:T(8,128)} %m_ref.1, f32[256,2048]{1,0:T(8,128)} %s_ref.1), custom_call_target="tpu_custom_call" | custom-call | tf_op jit(solution)/shard_map/pallas_call | solution.py:518
  130.6 0.6 reshape.254
  (36 shorter events, 0.2 us)
Async XLA Ops:
  2.0 1.9 %copy-start = (bf16[6144,256]{1,0:T(8,128)(2,1)S(1)}, bf16[6144,256]{1,0:T(8,128)(2,1)}, u32[]{:S(2)}) copy-start(bf16[6144,256]{1,0:T(8,128)(2,1)} %x_ref.3) | copy-start | bytes 9437188
  3.9 1.6 %copy-start.2 = (f32[256,2048]{1,0:T(8,128)S(1)}, f32[256,2048]{1,0:T(8,128)}, u32[]{:S(2)}) copy-start(f32[256,2048]{1,0:T(8,128)} %w_ref.3) | copy-start | bytes 6291460
  5.4 0.7 copy-start.5
  6.1 34.2 %copy-start.9 = (s32[6144]{0:T(1024)S(1)}, s32[6144]{0:T(1024)}, u32[]{:S(2)}) copy-start(s32[6144]{0:T(1024)} %param.16) | copy-start | bytes 73732
  6.1 34.3 %copy-start.10 = (s32[6144]{0:T(1024)S(1)}, s32[6144]{0:T(1024)}, u32[]{:S(2)}) copy-start(s32[6144]{0:T(1024)} %param.17) | copy-start | bytes 73732
  6.2 34.3 %copy-start.16 = (s32[1,16]{1,0:T(1,128)S(1)}, s32[1,16]{1,0:T(1,128)}, u32[]{:S(2)}) copy-start(s32[1,16]{1,0:T(1,128)} %param.18) | copy-start | bytes 196
  6.2 35.8 %copy-start.15 = (s32[12]{0:T(128)S(1)}, s32[12]{0:T(128)}, u32[]{:S(2)}) copy-start(s32[12]{0:T(128)} %param.19) | copy-start | bytes 148
  6.2 36.0 %copy-start.8 = (f32[12,512]{1,0:T(8,128)S(1)}, f32[12,512]{1,0:T(8,128)}, u32[]{:S(2)}) copy-start(f32[12,512]{1,0:T(8,128)} %param.20) | copy-start | bytes 73732
  6.2 64.4 %copy-start.1 = (bf16[6144,256]{1,0:T(8,128)(2,1)S(1)}, bf16[6144,256]{1,0:T(8,128)(2,1)}, u32[]{:S(2)}) copy-start(bf16[6144,256]{1,0:T(8,128)(2,1)} %x_ref.3) | copy-start | bytes 9437188
  42.2 1.2 copy-start.4
  70.6 52.4 %copy-start.7 = (f32[2048]{0:T(1024)S(1)}, f32[2048]{0:T(1024)}, u32[]{:S(2)}) copy-start(f32[2048]{0:T(1024)} %param.23) | copy-start | bytes 24580
  70.6 52.4 %copy-start.11 = (f32[2048]{0:T(1024)S(1)}, f32[2048]{0:T(1024)}, u32[]{:S(2)}) copy-start(f32[2048]{0:T(1024)} %param.28) | copy-start | bytes 24580
  70.6 52.4 %copy-start.12 = (f32[2048]{0:T(1024)S(1)}, f32[2048]{0:T(1024)}, u32[]{:S(2)}) copy-start(f32[2048]{0:T(1024)} %param.29) | copy-start | bytes 24580
  70.7 53.1 %copy-start.6 = (f32[2048]{0:T(1024)S(1)}, f32[2048]{0:T(1024)}, u32[]{:S(2)}) copy-start(f32[2048]{0:T(1024)} %param.22) | copy-start | bytes 24580
  70.7 53.0 %copy-start.13 = (f32[2048]{0:T(1024)S(1)}, f32[2048]{0:T(1024)}, u32[]{:S(2)}) copy-start(f32[2048]{0:T(1024)} %param.26) | copy-start | bytes 24580
  70.7 53.0 %copy-start.14 = (f32[2048]{0:T(1024)S(1)}, f32[2048]{0:T(1024)}, u32[]{:S(2)}) copy-start(f32[2048]{0:T(1024)} %param.27) | copy-start | bytes 24580
  122.0 1.0 copy-start.3

commit v3 on v2

--- a/solution.py
+++ b/solution.py
@@ -23,13 +23,47 @@
 F32 = jnp.float32
 
 
-def fwd_kernel(x_ref, w_ref, b_ref, wo_ref, h_ref, g_ref, s_ref, w_low):
-    @pl.when(pl.program_id(0) == 0)
+def split_three(values):
+    first = values.astype(BF)
+    rest = values - first.astype(F32)
+    second = rest.astype(BF)
+    third = (rest - second.astype(F32)).astype(BF)
+    return first, second, third
+
+
+def score_kernel(
+    n, cores, scale, x_ref, w_ref, b_ref, wo_ref, slot_ref, gain_ref, keep_ref, weight_ref,
+    h_ref, g_ref, doc_ref, lam_ref,
+    w_low, msg_ref, arrive, lam_out, lam_in, s_row, l_row, s_col, g_col, lam_t,
+    send_a, recv_a, send_l, recv_l,
+):
+    me = lax.axis_index("dp")
+    core = lax.axis_index("mp")
+    high_rows = gain_ref.shape[0]
+    per_list = weight_ref.shape[0]
+    lists = high_rows // per_list
+    cap = msg_ref.shape[2]
+    step = pl.program_id(0)
+    barrier = pltpu.get_barrier_semaphore()
+
+    @pl.when(step == 0)
     def _():
+        @pl.loop(1, n)
+        def _(k):
+            peer = lax.rem(me + k, n)
+            for d in range(cores):
+                pl.semaphore_signal(
+                    barrier, inc=1, device_id=(peer, lax.rem(core + d, cores)), device_id_type=MESH
+                )
+
+        for d in range(1, cores):
+            pl.semaphore_signal(
+                barrier, inc=1, device_id=(me, lax.rem(core + d, cores)), device_id_type=MESH
+            )
         w_low[...] = w_ref[...].astype(BF)
 
     x = x_ref[...]
-    acc = jnp.zeros((x.shape[0], LANES), F32)
+    acc = jnp.zeros((cap, LANES), F32)
     for k in range(h_ref.shape[0]):
         cols = slice(k * WIDE, (k + 1) * WIDE)
         v = jnp.dot(x, w_low[:, cols], preferred_element_type=F32) + b_ref[:, cols]
@@ -42,74 +76,12 @@
         h_ref[k] = hb
         g_ref[k] = g.astype(BF)
         acc = acc + jnp.dot(hb, wo_ref[cols, :], preferred_element_type=F32)
-    s_ref[0] = jnp.sum(acc.T, axis=0, keepdims=True)
-
-
-def forward(rows, weights, bias, wo_pair):
-    total, features = rows.shape
-    hidden = weights.shape[1]
-    blocks = total // BLOCK
-    groups = hidden // WIDE
-    return pl.pallas_call(
-        fwd_kernel,
-        grid=(blocks,),
-        in_specs=[
-            pl.BlockSpec((BLOCK, features), lambda i: (i, 0)),
-            pl.BlockSpec((features, hidden), lambda i: (0, 0)),
-            pl.BlockSpec((1, hidden), lambda i: (0, 0)),
-            pl.BlockSpec((hidden, LANES), lambda i: (0, 0)),
-        ],
-        out_specs=[
-            pl.BlockSpec((groups, BLOCK, WIDE), lambda i: (0, i, 0)),
-            pl.BlockSpec((groups, BLOCK, WIDE), lambda i: (0, i, 0)),
-            pl.BlockSpec((1, 1, BLOCK), lambda i: (i, 0, 0)),
-        ],
-        out_shape=[
-            jax.ShapeDtypeStruct((groups, total, WIDE), BF),
-            jax.ShapeDtypeStruct((groups, total, WIDE), BF),
-            jax.ShapeDtypeStruct((blocks, 1, BLOCK), F32),
-        ],
-        scratch_shapes=[pltpu.VMEM((features, hidden), BF)],
-        compiler_params=pltpu.CompilerParams(vmem_limit_bytes=48 << 20),
-    )(rows, weights, bias, wo_pair)
-
-
-def split_three(values):
-    first = values.astype(BF)
-    rest = values - first.astype(F32)
-    second = rest.astype(BF)
-    third = (rest - second.astype(F32)).astype(BF)
-    return first, second, third
-
-
-def mid_kernel(
-    n, cores, scale, msg_ref, gain_ref, keep_ref, weight_ref,
-    doc_ref, lam_ref,
-    arrive, lam_out, lam_in, s_row, l_row, s_col, g_col, lam_t,
-    send_a, recv_a, send_l, recv_l,
-):
-    me = lax.axis_index("dp")
-    core = lax.axis_index("mp")
-    high_rows = gain_ref.shape[0]
-    per_list = weight_ref.shape[0]
-    lists = high_rows // per_list
-    cap = msg_ref.shape[2]
-
-    barrier = pltpu.get_barrier_semaphore()
-
-    @pl.loop(1, n)
-    def _(k):
-        peer = lax.rem(me + k, n)
-        for d in range(cores):
-            pl.semaphore_signal(
-                barrier, inc=1, device_id=(peer, lax.rem(core + d, cores)), device_id_type=MESH
-            )
-
-    for d in range(1, cores):
-        pl.semaphore_signal(
-            barrier, inc=1, device_id=(me, lax.rem(core + d, cores)), device_id_type=MESH
-        )
-    pl.semaphore_wait(barrier, cores * n - 1)
+    msg_ref[step, 0:1, :] = jnp.sum(acc.T, axis=0, keepdims=True)
+    msg_ref[step, 1:3, :] = slot_ref[0]
+
+    @pl.when(step == 0)
+    def _():
+        pl.semaphore_wait(barrier, cores * n - 1)
 
     def score_copy(peer, d):
         return pltpu.make_async_remote_copy(
@@ -131,150 +103,172 @@
             device_id_type=MESH,
         )
 
-    @pl.loop(1, n)
-    def _(k):
-        peer = lax.rem(me + k, n)
-        for d in range(cores):
-            score_copy(peer, d).start()
+    def finish():
+        arrive[core, me] = msg_ref[me]
+        high_iota = lax.broadcasted_iota(jnp.int32, (LANES, cap), 0).astype(F32)
+
+        def absorb(shard, total):
+            first = arrive[0, shard]
+            value = first[0:1]
+            for c in range(1, cores):
+                value = value + arrive[c, shard][0:1]
+            low = (first[2:3] == high_iota).astype(F32).astype(BF)
+            at_high = first[1:2] == high_iota[:high_rows]
+            spread = jnp.concatenate(
+                [jnp.where(at_high, piece.astype(F32), 0.0).astype(BF) for piece in split_three(value)],
+                axis=0,
+            )
+            sums = lax.dot_general(
+                spread, low, (((1,), (1,)), ((), ())), preferred_element_type=F32
+            )
+            return total + (
+                sums[:high_rows] + sums[high_rows : 2 * high_rows] + sums[2 * high_rows :]
+            )
+
+        for d in range(1, cores):
+            arrival(lax.rem(core + d, cores), me).wait_recv()
+        total = absorb(me, jnp.zeros((high_rows, LANES), F32))
+
+        def take(k, total):
+            for j in range(3):
+                for c in range(cores):
+                    arrival(c, lax.rem(me + 1 + 3 * k + j, n)).wait_recv()
+            for j in range(3):
+                total = absorb(lax.rem(me + 1 + 3 * k + j, n), total)
+            return total
+
+        total = lax.fori_loop(0, (n - 1) // 3, take, total)
+        scores = jnp.where(keep_ref[...] > 0.0, 0.5 * total, -1e30)
+        s_row[...] = scores
+        padding = jnp.zeros((LANES - high_rows, LANES), F32)
+        s_turn = jnp.concatenate([scores, padding], axis=0).T
+        g_turn = jnp.concatenate([gain_ref[...], padding], axis=0).T
+        for i in range(high_rows):
+            s_col[i] = s_turn[:, i : i + 1]
+            g_col[i] = g_turn[:, i : i + 1]
+
+        def one_list(q, carry):
+            base = q * per_list
+            row_s = jnp.concatenate([s_row[pl.ds(base + k, 1), :] for k in range(per_list)], axis=1)
+            row_g = jnp.concatenate([gain_ref[pl.ds(base + k, 1), :] for k in range(per_list)], axis=1)
+            sums = jnp.zeros((8, row_s.shape[1]), F32)
+            for k in range(per_list):
+                col_s = s_col[base + k]
+                col_g = g_col[base + k]
+                for r in range(0, LANES, 8):
+                    delta_g = col_g[r : r + 8] - row_g
+                    delta_t = jnp.tanh(col_s[r : r + 8] - row_s)
+                    sums = sums + weight_ref[k, r : r + 8, :] * (delta_g - jnp.abs(delta_g) * delta_t)
+            lam = 0.5 * jnp.sum(sums, axis=0, keepdims=True)
+            for k in range(per_list):
+                l_row[pl.ds(base + k, 1), :] = lam[:, k * LANES : (k + 1) * LANES]
+            return carry
+
+        lax.fori_loop(0, lists, one_list, 0)
+        doc_ref[...] = l_row[...]
+        turned = jnp.concatenate([l_row[...] * scale, padding], axis=0).T
+        lam_t[...] = jnp.concatenate(split_three(turned), axis=1)
+
+        def answer(shard):
+            info = arrive[core, shard]
+            low = info[2:3] == high_iota
+            high = (info[1:2] == high_iota).astype(F32).astype(BF)
+            spread = jnp.dot(
+                lam_t[...], jnp.concatenate([high] * 3, axis=0), preferred_element_type=F32
+            )
+            return jnp.sum(jnp.where(low, spread, 0.0), axis=0, keepdims=True)
+
+        def lam_copy(peer):
+            return pltpu.make_async_remote_copy(
+                src_ref=lam_out.at[peer],
+                dst_ref=lam_in.at[me],
+                send_sem=send_l.at[peer],
+                recv_sem=recv_l.at[me],
+                device_id=(peer, core),
+                device_id_type=MESH,
+            )
+
+        def lam_arrival(peer):
+            return pltpu.make_async_remote_copy(
+                src_ref=lam_out.at[peer],
+                dst_ref=lam_in.at[peer],
+                send_sem=send_l.at[peer],
+                recv_sem=recv_l.at[peer],
+                device_id=(peer, core),
+                device_id_type=MESH,
+            )
+
+        @pl.loop(0, (n - 1) // 3)
+        def _(k):
+            peers = [lax.rem(me + 1 + 3 * k + j, n) for j in range(3)]
+            replies = [answer(peer) for peer in peers]
+            for peer, reply in zip(peers, replies):
+                lam_out[peer] = reply
+            for peer in peers:
+                lam_copy(peer).start()
+
+        lam_ref[me] = answer(me)
+
+        @pl.loop(1, n)
+        def _(k):
+            peer = lax.rem(me + k, n)
+            lam_arrival(peer).wait_recv()
+            lam_ref[peer] = lam_in[peer]
+
+        @pl.loop(1, n)
+        def _(k):
+            peer = lax.rem(me + k, n)
+            for d in range(cores):
+                score_copy(peer, d).wait_send()
+            lam_copy(peer).wait_send()
+
+        for d in range(1, cores):
+            score_copy(me, d).wait_send()
 
     for d in range(1, cores):
-        score_copy(me, d).start()
-    arrive[core, me] = msg_ref[me]
-
-    high_iota = lax.broadcasted_iota(jnp.int32, (LANES, cap), 0).astype(F32)
-
-    def absorb(shard, total):
-        first = arrive[0, shard]
-        value = first[0:1]
-        for c in range(1, cores):
-            value = value + arrive[c, shard][0:1]
-        low = (first[2:3] == high_iota).astype(F32).astype(BF)
-        at_high = first[1:2] == high_iota[:high_rows]
-        spread = jnp.concatenate(
-            [jnp.where(at_high, piece.astype(F32), 0.0).astype(BF) for piece in split_three(value)],
-            axis=0,
-        )
-        sums = lax.dot_general(
-            spread, low, (((1,), (1,)), ((), ())), preferred_element_type=F32
-        )
-        return total + (
-            sums[:high_rows] + sums[high_rows : 2 * high_rows] + sums[2 * high_rows :]
-        )
-
-    for d in range(1, cores):
-        arrival(lax.rem(core + d, cores), me).wait_recv()
-    total = absorb(me, jnp.zeros((high_rows, LANES), F32))
-
-    def take(k, total):
-        for j in range(3):
-            for c in range(cores):
-                arrival(c, lax.rem(me + 1 + 3 * k + j, n)).wait_recv()
-        for j in range(3):
-            total = absorb(lax.rem(me + 1 + 3 * k + j, n), total)
-        return total
-
-    total = lax.fori_loop(0, (n - 1) // 3, take, total)
-    scores = jnp.where(keep_ref[...] > 0.0, 0.5 * total, -1e30)
-    s_row[...] = scores
-    padding = jnp.zeros((LANES - high_rows, LANES), F32)
-    s_turn = jnp.concatenate([scores, padding], axis=0).T
-    g_turn = jnp.concatenate([gain_ref[...], padding], axis=0).T
-    for i in range(high_rows):
-        s_col[i] = s_turn[:, i : i + 1]
-        g_col[i] = g_turn[:, i : i + 1]
-
-    def one_list(q, carry):
-        base = q * per_list
-        row_s = jnp.concatenate([s_row[pl.ds(base + k, 1), :] for k in range(per_list)], axis=1)
-        row_g = jnp.concatenate([gain_ref[pl.ds(base + k, 1), :] for k in range(per_list)], axis=1)
-        sums = jnp.zeros((8, row_s.shape[1]), F32)
-        for k in range(per_list):
-            col_s = s_col[base + k]
-            col_g = g_col[base + k]
-            for r in range(0, LANES, 8):
-                delta_g = col_g[r : r + 8] - row_g
-                delta_t = jnp.tanh(col_s[r : r + 8] - row_s)
-                sums = sums + weight_ref[k, r : r + 8, :] * (delta_g - jnp.abs(delta_g) * delta_t)
-        lam = 0.5 * jnp.sum(sums, axis=0, keepdims=True)
-        for k in range(per_list):
-            l_row[pl.ds(base + k, 1), :] = lam[:, k * LANES : (k + 1) * LANES]
-        return carry
-
-    lax.fori_loop(0, lists, one_list, 0)
-    doc_ref[...] = l_row[...]
-    turned = jnp.concatenate([l_row[...] * scale, padding], axis=0).T
-    lam_t[...] = jnp.concatenate(split_three(turned), axis=1)
-
-    def answer(shard):
-        info = arrive[core, shard]
-        low = info[2:3] == high_iota
-        high = (info[1:2] == high_iota).astype(F32).astype(BF)
-        spread = jnp.dot(
-            lam_t[...], jnp.concatenate([high] * 3, axis=0), preferred_element_type=F32
-        )
-        return jnp.sum(jnp.where(low, spread, 0.0), axis=0, keepdims=True)
-
-    def lam_copy(peer):
-        return pltpu.make_async_remote_copy(
-            src_ref=lam_out.at[peer],
-            dst_ref=lam_in.at[me],
-            send_sem=send_l.at[peer],
-            recv_sem=recv_l.at[me],
-            device_id=(peer, core),
-            device_id_type=MESH,
-        )
-
-    def lam_arrival(peer):
-        return pltpu.make_async_remote_copy(
-            src_ref=lam_out.at[peer],
-            dst_ref=lam_in.at[peer],
-            send_sem=send_l.at[peer],
-            recv_sem=recv_l.at[peer],
-            device_id=(peer, core),
-            device_id_type=MESH,
-        )
-
-    @pl.loop(0, (n - 1) // 3)
-    def _(k):
-        peers = [lax.rem(me + 1 + 3 * k + j, n) for j in range(3)]
-        replies = [answer(peer) for peer in peers]
-        for peer, reply in zip(peers, replies):
-            lam_out[peer] = reply
-        for peer in peers:
-            lam_copy(peer).start()
-
-    lam_ref[me] = answer(me)
-
-    @pl.loop(1, n)
-    def _(k):
-        peer = lax.rem(me + k, n)
-        lam_arrival(peer).wait_recv()
-        lam_ref[peer] = lam_in[peer]
-
-    @pl.loop(1, n)
-    def _(k):
-        peer = lax.rem(me + k, n)
-        for d in range(cores):
-            score_copy(peer, d).wait_send()
-        lam_copy(peer).wait_send()
-
-    for d in range(1, cores):
-        score_copy(me, d).wait_send()
-
-
-def middle(n, cores, message, gain_rows, keep_rows, weights, query_total):
-    cap = message.shape[2]
+        score_copy(step, d).start()
+
+    @pl.when(step != me)
+    def _():
+        score_copy(step, 0).start()
+
+    pl.when(step == n - 1)(finish)
+
+
+def score(n, cores, rows, weights, bias, wo_pair, slots, gain_rows, keep_rows, pair_weights, total_lists):
+    total, features = rows.shape
+    hidden = weights.shape[1]
+    groups = hidden // WIDE
+    cap = total // n
     high_rows = gain_rows.shape[0]
-    vmem = pl.BlockSpec(memory_space=pltpu.VMEM)
+
+    def whole(array):
+        return pl.BlockSpec(array.shape, lambda i: (0,) * array.ndim)
+
+    block = pl.BlockSpec((groups, cap, WIDE), lambda i: (0, i, 0))
+    kept = jax.ShapeDtypeStruct((groups, total, WIDE), BF)
     return pl.pallas_call(
-        functools.partial(mid_kernel, n, cores, 1.0 / query_total),
-        in_specs=[vmem] * 4,
-        out_specs=[vmem] * 2,
+        functools.partial(score_kernel, n, cores, 1.0 / total_lists),
+        grid=(n,),
+        in_specs=[
+            pl.BlockSpec((cap, features), lambda i: (i, 0)),
+            whole(weights), whole(bias), whole(wo_pair),
+            pl.BlockSpec((1, 2, cap), lambda i: (i, 0, 0)),
+            whole(gain_rows), whole(keep_rows), whole(pair_weights),
+        ],
+        out_specs=[
+            block, block,
+            pl.BlockSpec((high_rows, LANES), lambda i: (0, 0)),
+            pl.BlockSpec((n, 1, cap), lambda i: (0, 0, 0)),
+        ],
         out_shape=[
+            kept, kept,
             jax.ShapeDtypeStruct((high_rows, LANES), F32),
             jax.ShapeDtypeStruct((n, 1, cap), F32),
         ],
         scratch_shapes=[
+            pltpu.VMEM((features, hidden), BF),
+            pltpu.VMEM((n, 3, cap), F32),
             pltpu.VMEM((cores, n, 3, cap), F32),
             pltpu.VMEM((n, 1, cap), F32),
             pltpu.VMEM((n, 1, cap), F32),
@@ -291,7 +285,7 @@
         compiler_params=pltpu.CompilerParams(
             collective_id=0, has_side_effects=True, vmem_limit_bytes=48 << 20
         ),
-    )(message, gain_rows, keep_rows, weights)
+    )(rows, weights, bias, wo_pair, slots, gain_rows, keep_rows, pair_weights)
 
 
 def tail_rows(grad_b, grad_o):
@@ -558,10 +552,9 @@
         lane == 0, wo_top[:, None], jnp.where(lane == 1, wo_rest[:, None], jnp.zeros((), BF))
     )
 
-    hid, slope, scores = forward(log_rows, weight_in, bias_in.reshape(1, hidden), wo_pair)
-    message = jnp.stack([scores.reshape(n, cap), high, low], axis=1)
-    doc_rows, lam = middle(
-        n, lax.axis_size("mp"), message, gain_rows, keep_rows, weights, list_count * n
+    hid, slope, doc_rows, lam = score(
+        n, lax.axis_size("mp"), log_rows, weight_in, bias_in.reshape(1, hidden), wo_pair,
+        jnp.stack([high, low], axis=1), gain_rows, keep_rows, weights, list_count * n,
     )
     lambdas = doc_rows.reshape(list_count, list_width)
 

time: 132 us -> 125 us (0.947)
  local copies, waits for them, and re-layouts: 7.26 us -> 1.67 us
  Pallas kernels: 119 us -> 117 us
    unnamed x34 -> x18, local copies, waits for them, and re-layouts: 6.47 us -> 0.05 us
    pallas_call x2 -> x1, Pallas kernels: 61.3 us -> 59.4 us  [score(): pl.pallas_call(functools.partial(score_kernel, n, cores, 1.0 / total_list...]
where the time goes in v3:
time: 125 us
  Pallas kernels  117 us (94%)
  other arithmetic  5.44 us (4%)
  local copies, waits for them, and re-layouts  1.67 us (1%)
    pallas_call x1, Pallas kernels, score(): pl.pallas_call(functools.partial(score_kernel, n, cores, 1.0 / total_list...  59.4 us
    pallas_call x1, Pallas kernels, gradients(): pl.pallas_call(functools.partial(grad_kernel, n, parts_per_span), in_spec...  51.2 us
    pallas_call x1, Pallas kernels, adam_matrix(): pl.pallas_call(adam_kernel, grid=(hidden // (group * LANES),), in_specs=[...  6.22 us

profile of v3, /device:TPU:0, one launch (start us, length us, event | category | flops | bytes accessed | tf_op | source)
XLA Modules:
  0.0 124.8 jit_solution(9920013727338543087)
XLA Ops:
  0.6 0.0 copy-start.3
  0.7 0.0 copy-start.1
  0.7 0.9 lt.82
  1.6 0.1 lt.83
  1.7 0.7 broadcast_multiply_fusion
  2.4 0.1 compare_convert_fusion.keep_ref
  2.5 0.8 broadcast_remainder_fusion
  3.2 0.9 fusion.1
  4.3 0.8 fusion
  5.1 0.6 select_select_fusion.wo_ref
  5.7 0.1 subtract_abs_fusion.weight_ref
  5.9 0.0 copy-done.3
  5.9 0.0 copy-start
  5.9 59.4 %shard_map.222 = (bf16[8,6144,256]{2,1,0:T(8,128)(2,1)}, bf16[8,6144,256]{2,1,0:T(8,128)(2,1)}, f32[48,128]{1,0:T(8,128)S(1)}, f32[16,1,384]{2,1,0:T(1,128)S(1)}) custom-call(bf16[6144,256]{1,0:T(8,128)(2,1)} %x_ref.3, f32[256,2048]{1,0:T(8,128)S(1)} %copy-done.1, f32[1,2048]{1,0:T(1,128)S(1)} %bitcast.9, bf16[2048,128]{1,0:T(8,128)(2,1)S(1)} %select_select_fusion.wo_ref, ...), custom_call_target="tpu_custom_call" | custom-call | tf_op jit(solution)/shard_map/pallas_call | solution.py:250
  65.3 0.0 copy-start.5
  65.3 0.0 copy-start.6
  65.4 0.0 copy-start.4
  65.4 0.0 copy-start.7
  65.4 0.0 copy-start.8
  65.4 51.2 %shard_map.223.g_ref = bf16[16,272,128]{2,1,0:T(8,128)(2,1)S(1)} custom-call(bf16[6144,256]{1,0:T(8,128)(2,1)S(1)} %copy-done, f32[12,1,512]{2,1,0:T(1,128)S(1)} %bitcast.11, f32[8,1,256]{2,1,0:T(1,128)S(1)} %bitcast.10, bf16[8,6144,256]{2,1,0:T(8,128)(2,1)} %get-tuple-element.19.h_hbm, bf16[8,6144,256]{2,1,0:T(8,128)(2,1)} %get-tuple-element.20.g_hbm), custom_call_target="tpu_custom_call" | custom-call | tf_op jit(solution)/shard_map/pallas_call | solution.py:466
  116.6 0.7 reshape.254
  117.3 0.6 divide_subtract_fusion.1
  118.0 0.6 divide_subtract_fusion
  118.6 6.2 %shard_map.224 = (f32[256,2048]{1,0:T(8,128)}, f32[256,2048]{1,0:T(8,128)}, f32[256,2048]{1,0:T(8,128)}) custom-call(bf16[16,272,128]{2,1,0:T(8,128)(2,1)} %copy-done.2, f32[256,2048]{1,0:T(8,128)} %w_ref.3, f32[256,2048]{1,0:T(8,128)} %m_ref.1, f32[256,2048]{1,0:T(8,128)} %s_ref.1), custom_call_target="tpu_custom_call" | custom-call | tf_op jit(solution)/shard_map/pallas_call | solution.py:512
  (19 shorter events, 0.2 us)
Async XLA Ops:
  0.6 5.2 %copy-start.3 = (f32[2048]{0:T(1024)S(1)}, f32[2048]{0:T(1024)}, u32[]{:S(2)}) copy-start(f32[2048]{0:T(1024)} %param.22) | copy-start | bytes 24580
  0.7 5.2 %copy-start.1 = (f32[256,2048]{1,0:T(8,128)S(1)}, f32[256,2048]{1,0:T(8,128)}, u32[]{:S(2)}) copy-start(f32[256,2048]{1,0:T(8,128)} %w_ref.3) | copy-start | bytes 6291460
  5.9 59.4 %copy-start = (bf16[6144,256]{1,0:T(8,128)(2,1)S(1)}, bf16[6144,256]{1,0:T(8,128)(2,1)}, u32[]{:S(2)}) copy-start(bf16[6144,256]{1,0:T(8,128)(2,1)} %x_ref.3) | copy-start | bytes 9437188
  65.3 52.0 %copy-start.5 = (f32[2048]{0:T(1024)S(1)}, f32[2048]{0:T(1024)}, u32[]{:S(2)}) copy-start(f32[2048]{0:T(1024)} %param.26) | copy-start | bytes 24580
  65.3 52.0 %copy-start.6 = (f32[2048]{0:T(1024)S(1)}, f32[2048]{0:T(1024)}, u32[]{:S(2)}) copy-start(f32[2048]{0:T(1024)} %param.27) | copy-start | bytes 24580
  65.4 52.6 %copy-start.4 = (f32[2048]{0:T(1024)S(1)}, f32[2048]{0:T(1024)}, u32[]{:S(2)}) copy-start(f32[2048]{0:T(1024)} %param.23) | copy-start | bytes 24580
  65.4 52.6 %copy-start.7 = (f32[2048]{0:T(1024)S(1)}, f32[2048]{0:T(1024)}, u32[]{:S(2)}) copy-start(f32[2048]{0:T(1024)} %param.28) | copy-start | bytes 24580
  65.4 52.6 %copy-start.8 = (f32[2048]{0:T(1024)S(1)}, f32[2048]{0:T(1024)}, u32[]{:S(2)}) copy-start(f32[2048]{0:T(1024)} %param.29) | copy-start | bytes 24580
  116.6 2.0 %copy-start.2 = (bf16[16,272,128]{2,1,0:T(8,128)(2,1)}, bf16[16,272,128]{2,1,0:T(8,128)(2,1)S(1)}, u32[]{:S(2)}) copy-start(bf16[16,272,128]{2,1,0:T(8,128)(2,1)S(1)} %shard_map.223.g_ref) | copy-start | bytes 3342340
